TPU v7x, 32 devices: a whole 2x2x4 slice. The times are simulated.
32 devices in a mesh: grp: 4 (over y, x), dev: 8 (over z, core).
Axes of the slice: x: 2, y: 2, z: 4, core: 2. Of those that a mesh axis runs over, the one named last changes fastest.
Arguments:
- queries: bfloat16 [4096, 256], P(('grp', 'dev')), may hold values from -32 to 32
- items: bfloat16 [4096, 256], P(('grp', 'dev')), may hold values from -24 to 24
- item_ids: int32 [4096], P('grp'), may hold values from 0 to 262143
- neg_embed: bfloat16 [4096, 256], P('dev'), may hold values from -6 to 6
- neg_logq: float32 [4096], P('dev'), may hold values from -12 to -8
- logq_table: float32 [262144], replicated, may hold values from -11 to -9.5
Outputs:
- query_loss: float32 [4096], P(('grp', 'dev'))
- query_grad: float32 [4096, 256], P(('grp', 'dev'))
- item_grad: float32 [4096, 256], P(('grp', 'dev'))
- negative_grad: float32 [4096, 256], P('dev')
Inputs may be any that keep to these rules, and one draw needn't show every extreme that they name: `item_ids`: a row of logq_table.
All inputs are finite; a program needn't handle non-finite values.
Results may differ from a plain program's by a relative error of at most 0.0036.
Values may be sent and summed in bfloat16 or wider, within the bound.
No kernel may reach another device: no remote copies, remote signals or barrier semaphores. Data moves between devices by JAX's collectives and lax.ppermute only.
A program may use at most 64 MiB of HBM per device.

v0:
```python
import jax
import jax.numpy as jnp
from jax import lax
from jax.sharding import PartitionSpec as P

logit_scale = 0.25


def block_shape(all_rows):
    block_rows = min(512, all_rows)
    return (block_rows, all_rows // block_rows)


def log_total(maxima, totals):
    row_max = lax.pmax(maxima, "dev")
    row_sum = lax.psum(totals * jnp.exp(maxima - row_max), "dev")
    return row_max + jnp.log(row_sum)


def row_stats(scores):
    row_max = jnp.max(scores, axis=1)
    return (row_max, jnp.sum(jnp.exp(scores - row_max[:, None]), axis=1))


def logits(q_block, candidates, cand_offsets):
    return (
        logit_scale * jnp.dot(q_block, candidates.T, preferred_element_type=jnp.float32)
        - cand_offsets[None, :]
    )


def local(queries, items, item_ids, neg_embed, neg_logq, logq_table):
    own_rows, feat_width = queries.shape
    dev_index = lax.axis_index("dev")
    own_start = dev_index * own_rows
    own_ids = lax.dynamic_slice_in_dim(item_ids, own_start, own_rows, 0)
    own_offsets = jnp.take(logq_table, own_ids, axis=0)
    group_q = lax.all_gather(queries, "dev", axis=0, tiled=True)
    all_rows = group_q.shape[0]
    block_rows, block_count = block_shape(all_rows)
    blocks = group_q.reshape(block_count, block_rows, feat_width)
    starts = jnp.arange(block_count, dtype=jnp.int32) * block_rows
    candidates = jnp.concatenate([items, neg_embed], axis=0)
    cand_offsets = jnp.concatenate([own_offsets, neg_logq], axis=0)
    columns = jnp.arange(candidates.shape[0], dtype=jnp.int32)

    def positives(first_row):
        targets = first_row + jnp.arange(block_rows, dtype=jnp.int32) - own_start
        return (columns[None, :] == targets[:, None]) & (columns[None, :] < own_rows)

    def forward(packed):
        q_block, first_row = packed
        scores = logits(q_block, candidates, cand_offsets)
        row_max, row_sum = row_stats(scores)
        return (row_max, row_sum, jnp.sum(jnp.where(positives(first_row), scores, 0.0), axis=1))

    maxima, totals, matched = lax.map(forward, (blocks, starts))
    log_norm = log_total(maxima.reshape(all_rows), totals.reshape(all_rows))
    own_norm = lax.dynamic_slice_in_dim(log_norm, own_start, own_rows, 0)
    own_match = lax.dynamic_slice_in_dim(matched.reshape(all_rows), own_start, own_rows, 0)
    query_loss = own_norm - own_match

    def backward(summed, packed):
        q_block, first_row, block_norm = packed
        scores = logits(q_block, candidates, cand_offsets)
        logit_grad = (
            logit_scale
            * (jnp.exp(scores - block_norm[:, None]) - positives(first_row).astype(jnp.float32))
        ).astype(jnp.bfloat16)
        summed = summed + jnp.einsum(
            "rc,rd->cd", logit_grad, q_block, preferred_element_type=jnp.float32
        )
        return (summed, jnp.dot(logit_grad, candidates, preferred_element_type=jnp.float32))

    zero_acc = jnp.zeros((candidates.shape[0], feat_width), jnp.float32)
    cand_grad, q_partial = lax.scan(
        backward, zero_acc, (blocks, starts, log_norm.reshape(block_count, block_rows))
    )
    query_grad = lax.psum_scatter(
        q_partial.reshape(all_rows, feat_width), "dev", scatter_dimension=0, tiled=True
    )
    item_grad = cand_grad[:own_rows]
    negative_part = cand_grad[own_rows:]
    negative_grad = lax.psum(negative_part, "grp")
    return (query_loss, query_grad, item_grad, negative_grad)


def solution(mesh):
    return jax.shard_map(
        local,
        mesh=mesh,
        in_specs=(
            P(("grp", "dev"), None),
            P(("grp", "dev"), None),
            P("grp"),
            P("dev", None),
            P("dev"),
            P(),
        ),
        out_specs=(
            P(("grp", "dev")),
            P(("grp", "dev"), None),
            P(("grp", "dev"), None),
            P("dev", None),
        ),
        check_vma=False,
    )
```

profile of v0, /device:TPU:0, one launch (start us, length us, event | category | flops | bytes accessed | tf_op | source)
XLA Modules:
  0.0 128.1 jit_solution(7890898230688318742)
XLA Ops:
  8.1 0.8 compare_select_fusion
  9.2 1.1 gather_fusion
  10.4 0.8 and_select_fusion
  11.2 0.8 constant_dynamic-update-slice_fusion.1
  12.0 16.7 %all_gather.3 = bf16[1024,256]{1,0:T(8,128)(2,1)S(1)} all-gather(bf16[128,256]{1,0:T(8,128)(2,1)} %param.10), channel_id=1, replica_groups=mesh['grp'=4,'dev'=8] {'dev'}, dimensions={0}, use_global_device_ids=true | all-gather | bytes 589824 | tf_op jit(solution)/shard_map/all_gather | solution.py:38
  28.7 0.7 pad_maximum_fusion
  29.4 5.2 %while.30 = (s32[]{:T(128)}, f32[2,512]{1,0:T(2,128)S(1)}, f32[2,512]{1,0:T(2,128)S(1)}, f32[2,512]{1,0:T(2,128)S(1)}, bf16[2,512,256]{2,1,0:T(8,128)(2,1)S(1)},...) while((s32[]{:T(128)}, f32[2,512]{1,0:T(2,128)S(1)}, ...), condition=%wide.region_4.5_spmd.clone.clone, body=%wide.region_0.4_spmd.clone.clone.sunk | while | flops 170721408 | bytes 3241369 | solution.py:57
  29.4 0.6 dynamic_slice.67
  30.0 0.6 add_subtract_fusion.4
  31.2 0.7 select_reduce_fusion.2
  32.0 0.6 dynamic_slice.67
  32.6 0.6 add_subtract_fusion.4
  33.8 0.7 select_reduce_fusion.2
  34.6 17.0 %pmax.7 = f32[1024]{0:T(1024)S(1)} all-reduce(f32[1024]{0:T(1024)S(1)} %bitcast.69), channel_id=1, replica_groups=mesh['grp'=4,'dev'=8] {'dev'}, use_global_device_ids=true, to_apply=%region_5.6 | all-reduce | flops 1024 | bytes 8192 | tf_op jit(solution)/shard_map/pmax | solution.py:15
  51.6 13.6 %psum.14 = f32[1024]{0:T(1024)S(1)} all-reduce(f32[1024]{0:T(1024)S(1)} %exponential_multiply_fusion), channel_id=1, replica_groups=mesh['grp'=4,'dev'=8] {'dev'}, use_global_device_ids=true, to_apply=%region_6.7 | all-reduce | flops 1024 | bytes 8192 | tf_op jit(solution)/shard_map/psum | solution.py:16
  65.2 9.0 %while.31 = (s32[]{:T(128)}, f32[640,256]{1,0:T(8,128)S(1)}, f32[2,512,256]{2,1,0:T(8,128)}, bf16[2,512,256]{2,1,0:T(8,128)(2,1)S(1)}, bf16[640,256]{1,0:T(8,128...) while((s32[]{:T(128)}, f32[640,256]{1,0:T(8,128)S(1)}, ...), condition=%wide.region_8.9_spmd.clone.clone, body=%wide.region_7.8_spmd.clone.clone.sunk | while | flops 506594944 | bytes 13385563 | solution.py:76
  65.2 0.6 dynamic_slice.71
  65.8 0.6 add_subtract_fusion.5
  66.5 0.6 fusion.47
  67.7 0.7 copy-done.1
  68.7 1.0 copy-done.2
  69.7 0.6 dynamic_slice.71
  70.3 0.6 add_subtract_fusion.5
  71.0 0.6 fusion.47
  71.6 0.5 convolution_add_fusion.2
  72.2 0.7 copy-done.1
  73.2 1.0 copy-done.2
  74.2 0.8 slice.7
  75.7 0.7 slice.6
  76.3 0.6 dynamic-slice_subtract_fusion
  76.9 41.9 %all-reduce.2.cloned.1.call-done = f32[512,256]{1,0:T(8,128)} async-done(((f32[512,256]{1,0:T(8,128)}), f32[512,256]{1,0:T(8,128)}) %all-reduce.2.cloned.1.call-update) | async-done | bytes 524304 | tf_op jit(solution)/shard_map/psum | solution.py:84
  118.8 1.9 %copy.40 = f32[512,256]{1,0:T(8,128)} copy(f32[512,256]{1,0:T(8,128)} %all-reduce.2.cloned.1.call-done) | data formatting | bytes 1048576
  (44 shorter events, 3.5 us)
Async XLA Ops:
  8.0 1.2 copy-start
  8.0 21.4 %copy-start.3 = (bf16[512,256]{1,0:T(8,128)(2,1)S(1)}, bf16[512,256]{1,0:T(8,128)(2,1)}, u32[]{:S(2)}) copy-start(bf16[512,256]{1,0:T(8,128)(2,1)} %param.13) | copy-start | bytes 786436
  8.0 110.8 %all-reduce.2.cloned.1.call-start = ((), (), s32[]{:S(2)}) async-start(), calls=%async_computation.2 | async-start | bytes 1048576 | tf_op jit(solution)/shard_map/psum | solution.py:84
  67.1 1.2 copy-start.1
  68.7 1.0 copy-start.2
  71.6 1.2 copy-start.1
  73.2 1.0 copy-start.2
  75.1 43.7 %reduce-scatter.2.cloned.1.call-start = ((), (), s32[]{:S(2)}) async-start(), calls=%async_computation.1 | async-start | bytes 1179648 | tf_op jit(solution)/shard_map/reduce_scatter | solution.py:79
Sparse Core Ops, SparseCore 0:
  75.2 43.5 all-reduce.1
Sparse Core Ops, SparseCore 1:
  78.4 30.7 reduce-scatter.1
where the time goes:
time: 129 us; the launch traced here: 128 us
  blocking collectives  47.3 us (37%)
  waiting for transfers between devices  42.4 us (33%)
  between operations  15.6 us (12%)
  local copies, waits for them, and re-layouts  11.6 us (9%)
  other arithmetic  6.94 us (5%)
  matrix products  4.02 us (3%)
    psum x1, waiting for transfers between devices, local(): negative_grad = lax.psum(negative_part, 'grp')  41.9 us
    pmax x1, blocking collectives, log_total(): row_max = lax.pmax(maxima, 'dev')  17 us
    all_gather x1, blocking collectives, local(): group_q = lax.all_gather(queries, 'dev', axis=0, tiled=True)  16.7 us
    psum x1, blocking collectives, log_total(): row_sum = lax.psum(totals * jnp.exp(maxima - row_max), 'dev')  13.6 us
    while x8, local copies, waits for them, and re-layouts  3.35 us
    unnamed x9, local copies, waits for them, and re-layouts  2.99 us
    sub x4, other arithmetic, positives(): targets = first_row + jnp.arange(block_rows, dtype=jnp.int32) - own_start  2.59 us
  transfers between devices with their start and end apart: 2, of which 1 were waited for; matrix products, arithmetic and copies ran while one was open for 1% of the time, Pallas kernels for 0%

commit v1 on v0

v1 whole, which is shorter than its diff:
```python
import jax
import jax.numpy as jnp
from jax import lax
from jax.experimental import pallas as pl
from jax.experimental.pallas import tpu as pltpu
from jax.sharding import PartitionSpec as P

logit_scale = 0.25
VMEM = pl.BlockSpec(memory_space=pltpu.VMEM)
F32, BF16 = jnp.float32, jnp.bfloat16
NT = (((1,), (1,)), ((), ()))


def round_up(x, m):
    return -(-x // m) * m


def swap(x, axis, count, mask):
    return lax.ppermute(x, axis, [(i, i ^ mask) for i in range(count)])


def fold(x, op):
    rows, cols = x.shape
    return op(x.reshape(rows // 8, 8, cols), axis=0)


def pad_rows(parts, multiple):
    have = sum(p.shape[0] for p in parts)
    lack = round_up(have, multiple) - have
    if lack:
        parts = parts + [jnp.zeros((lack, parts[0].shape[1]), parts[0].dtype)]
    return jnp.concatenate(parts, axis=0)


def offset_columns(rows, pieces):
    flipped = pad_rows(rows, 8).T
    return [flipped[:, j : j + 1] for j in range(pieces)]


def split3(x):
    hi = x.astype(BF16)
    rest = x - hi.astype(F32)
    mid = rest.astype(BF16)
    return (hi, mid, (rest - mid.astype(F32)).astype(BF16))


def candidate_rows(refs, offs, rows):
    out = []
    for ref, off in zip(refs, offs):
        for j in range(ref.shape[0] // rows):
            out.append((ref, j * rows, off[j : j + 1, :]))
    return out


def forward_kernel(n, *refs):
    q_refs, refs = refs[:n], refs[n:]
    c_refs, refs = refs[:4], refs[4:]
    off_refs, refs = refs[:4], refs[4:]
    own_ref, lse_ref, msg_refs = refs[0], refs[1], refs[2 : 2 + n - 1]
    q_all, c_t, s_all, e_all = refs[2 + n - 1 :]
    rows, width = q_refs[0].shape
    runs = candidate_rows(c_refs, [r[...] for r in off_refs], rows)
    cols = offset_columns([r[2] for r in runs], len(runs))
    for k in range(n):
        q_all[k * rows : (k + 1) * rows, :] = q_refs[k][...]
    for j, (ref, first, _) in enumerate(runs):
        c_t[:, j * rows : (j + 1) * rows] = ref[first : first + rows, :].T
    per = 2 if n % 2 == 0 else 1
    chunk = per * rows
    for p in range(n // per):
        q = q_all[p * chunk : (p + 1) * chunk, :]
        top = None
        for j, (ref, first, _) in enumerate(runs):
            s = lax.dot_general(ref[first : first + rows, :], q, NT, preferred_element_type=F32)
            s = logit_scale * s - cols[j]
            s_all[j * rows : (j + 1) * rows, :] = s
            here = fold(s, jnp.max)
            top = here if top is None else jnp.maximum(top, here)
        row_max = jnp.max(top, axis=0, keepdims=True)
        total = None
        for j in range(len(runs)):
            e = jnp.exp(s_all[j * rows : (j + 1) * rows, :] - row_max)
            e_all[j * rows : (j + 1) * rows, :] = e.astype(BF16)
            here = fold(e, jnp.sum)
            total = here if total is None else total + here
        row_sum = jnp.sum(total, axis=0, keepdims=True)
        lse = row_max + jnp.log(row_sum)
        u = jnp.dot(c_t[...], e_all[...], preferred_element_type=F32) / row_sum
        for i in range(per):
            k = p * per + i
            lse_ref[k : k + 1, :] = lse[:, i * rows : (i + 1) * rows]
            u_k = u[:, i * rows : (i + 1) * rows]
            if k == 0:
                own_ref[...] = u_k
            else:
                msg_refs[k - 1][:width, :] = u_k.astype(BF16)
    parts = split3(lse_ref[...])
    block = pad_rows(list(parts), 16)
    for k in range(1, n):
        msg_refs[k - 1][width:, :] = block


def merged_lse(n, lse_ref, msg_refs, width):
    mine = lse_ref[...]
    all_lse = [mine]
    for k in range(1, n):
        got = msg_refs[k - 1][width:, :].astype(F32)
        all_lse.append(got[:n] + got[n : 2 * n] + got[2 * n : 3 * n])
    norms = []
    for b in range(n):
        rows = [all_lse[k][k ^ b : (k ^ b) + 1, :] for k in range(n)]
        top = rows[0]
        for r in rows[1:]:
            top = jnp.maximum(top, r)
        total = jnp.exp(rows[0] - top)
        for r in rows[1:]:
            total = total + jnp.exp(r - top)
        norms.append(top + jnp.log(total))
    return all_lse, norms


def gradient(n, q_all, runs, cols, norms, mask_first, e_all, emit):
    rows = q_all.shape[0] // n
    per = 2 if n % 2 == 0 else 1
    chunk = per * rows
    matched = None
    for j, (ref, first, _) in enumerate(runs):
        cand = ref[first : first + rows, :]
        for p in range(n // per):
            norm = jnp.concatenate(norms[p * per : (p + 1) * per], axis=1)
            q = q_all[p * chunk : (p + 1) * chunk, :]
            s = lax.dot_general(cand, q, NT, preferred_element_type=F32)
            s = logit_scale * s - cols[j]
            prob = jnp.exp(s - norm)
            if mask_first and j == 0 and p == 0:
                r = lax.broadcasted_iota(jnp.int32, s.shape, 0)
                c = lax.broadcasted_iota(jnp.int32, s.shape, 1)
                hit = r == c
                matched = jnp.sum(jnp.where(hit, s, 0.0), axis=0, keepdims=True)[:, :rows]
                prob = prob - hit.astype(F32)
            e_all[:, p * chunk : (p + 1) * chunk] = (logit_scale * prob).astype(BF16)
        emit(j, jnp.dot(e_all[...], q_all[...], preferred_element_type=F32))
    return matched


def partner_kernel(n, *refs):
    q_refs, refs = refs[:n], refs[n:]
    c_refs, refs = refs[:2], refs[2:]
    off_refs, refs = refs[:2], refs[2:]
    lse_ref, refs = refs[0], refs[1:]
    msg_refs, refs = refs[: n - 1], refs[n - 1 :]
    out_ref, q_all, e_all = refs
    rows, width = q_refs[0].shape
    for k in range(n):
        q_all[k * rows : (k + 1) * rows, :] = q_refs[k][...]
    runs = candidate_rows(c_refs, [r[...] for r in off_refs], rows)
    cols = offset_columns([r[2] for r in runs], len(runs))
    _, norms = merged_lse(n, lse_ref, msg_refs, width)

    def emit(j, g):
        out_ref[j * rows : (j + 1) * rows, :] = g.astype(BF16)

    gradient(n, q_all, runs, cols, norms, False, e_all, emit)


def own_kernel(n, *refs):
    q_refs, refs = refs[:n], refs[n:]
    c_refs, refs = refs[:2], refs[2:]
    off_refs, refs = refs[:2], refs[2:]
    lse_ref, own_ref, refs = refs[0], refs[1], refs[2:]
    msg_refs, refs = refs[: n - 1], refs[n - 1 :]
    loss_ref, qg_ref, item_ref, neg_ref, q_all, e_all = refs
    rows, width = q_refs[0].shape
    for k in range(n):
        q_all[k * rows : (k + 1) * rows, :] = q_refs[k][...]
    runs = candidate_rows(c_refs, [r[...] for r in off_refs], rows)
    cols = offset_columns([r[2] for r in runs], len(runs))
    all_lse, norms = merged_lse(n, lse_ref, msg_refs, width)

    def emit(j, g):
        if j == 0:
            item_ref[...] = g
        else:
            neg_ref[(j - 1) * rows : j * rows, :] = g

    matched = gradient(n, q_all, runs, cols, norms, True, e_all, emit)
    loss_ref[...] = norms[0] - matched
    total = jnp.exp(all_lse[0][0:1, :] - norms[0]) * own_ref[...]
    for k in range(1, n):
        weight = jnp.exp(all_lse[k][k : k + 1, :] - norms[0])
        total = total + weight * msg_refs[k - 1][:width, :].astype(F32)
    qg_ref[...] = logit_scale * (total.T - c_refs[0][...].astype(F32))


def local_fn(mesh):
    n_dev, n_grp = mesh.shape["dev"], mesh.shape["grp"]
    n = n_dev // 2

    def local(queries, items, item_ids, neg_embed, neg_logq, logq_table):
        rows, width = queries.shape
        negs = neg_embed.shape[0]
        dev = lax.axis_index("dev")
        q = [queries] + [swap(queries, "dev", n_dev, 2 * k) for k in range(1, n)]
        items_p = swap(items, "dev", n_dev, 1)
        neg_p = swap(neg_embed, "dev", n_dev, 1)
        logq_p = swap(neg_logq, "dev", n_dev, 1)
        pair_ids = lax.dynamic_slice_in_dim(item_ids, (dev // 2) * (2 * rows), 2 * rows, 0)
        pair_off = logq_table.at[pair_ids].get(mode="promise_in_bounds").reshape(2, rows)
        core = dev % 2
        off_o = lax.dynamic_slice_in_dim(pair_off, core, 1, 0)
        off_p = lax.dynamic_slice_in_dim(pair_off, 1 - core, 1, 0)
        lq_o = neg_logq.reshape(negs // rows, rows)
        lq_p = logq_p.reshape(negs // rows, rows)

        cands = 2 * (rows + negs)
        chunk = (2 if n % 2 == 0 else 1) * rows
        msg_rows = width + round_up(3 * n, 16)
        shape = jax.ShapeDtypeStruct
        pairs = cands * n * rows

        own_u, lse, *msgs = pl.pallas_call(
            lambda *r: forward_kernel(n, *r),
            name="fwd",
            out_shape=[shape((width, rows), F32), shape((n, rows), F32)]
            + [shape((msg_rows, rows), BF16)] * (n - 1),
            in_specs=[VMEM] * (n + 8),
            out_specs=[VMEM] * (n + 1),
            scratch_shapes=[
                pltpu.VMEM((n * rows, width), BF16),
                pltpu.VMEM((width, cands), BF16),
                pltpu.VMEM((cands, chunk), F32),
                pltpu.VMEM((cands, chunk), BF16),
            ],
            cost_estimate=pl.CostEstimate(
                flops=4 * pairs * width, bytes_accessed=4 * cands * width, transcendentals=pairs
            ),
        )(*q, items, items_p, neg_embed, neg_p, off_o, off_p, lq_o, lq_p)

        got = [swap(msgs[k - 1], "dev", n_dev, 2 * k) for k in range(1, n)]

        half_cost = pl.CostEstimate(
            flops=2 * pairs * width, bytes_accessed=4 * cands * width, transcendentals=pairs // 2
        )
        half_scratch = [
            pltpu.VMEM((n * rows, width), BF16),
            pltpu.VMEM((rows, n * rows), BF16),
        ]
        theirs = pl.pallas_call(
            lambda *r: partner_kernel(n, *r),
            name="partner",
            out_shape=shape((rows + negs, width), BF16),
            in_specs=[VMEM] * (2 * n + 4),
            out_specs=VMEM,
            scratch_shapes=half_scratch,
            cost_estimate=half_cost,
        )(*q, items_p, neg_p, off_p, lq_p, lse, *got)
        back = swap(theirs, "dev", n_dev, 1)
        loss, query_grad, item_part, neg_part = pl.pallas_call(
            lambda *r: own_kernel(n, *r),
            name="own",
            out_shape=[
                shape((1, rows), F32),
                shape((rows, width), F32),
                shape((rows, width), F32),
                shape((negs, width), F32),
            ],
            in_specs=[VMEM] * (2 * n + 5),
            out_specs=[VMEM] * 4,
            scratch_shapes=half_scratch,
            cost_estimate=half_cost,
        )(*q, items, neg_embed, off_o, lq_o, lse, own_u, *got)

        item_grad = item_part + back[:rows].astype(F32)
        total = neg_part + back[rows:].astype(F32)
        masks = [1 << i for i in range((n_grp - 1).bit_length())]
        steps = len(masks)
        share = negs // steps if steps and negs % (16 * steps) == 0 else negs
        parts = []
        for i in range(negs // share):
            part = total[i * share : (i + 1) * share]
            for t in range(steps):
                part = part.astype(BF16)
                other = swap(part, "grp", n_grp, masks[(i + t) % steps])
                part = part.astype(F32) + other.astype(F32)
            parts.append(part)
        negative_grad = jnp.concatenate(parts, axis=0) if len(parts) > 1 else parts[0]
        return (loss.reshape(rows), query_grad, item_grad, negative_grad)

    return local


def solution(mesh):
    return jax.shard_map(
        local_fn(mesh),
        mesh=mesh,
        in_specs=(
            P(("grp", "dev"), None),
            P(("grp", "dev"), None),
            P("grp"),
            P("dev", None),
            P("dev"),
            P(),
        ),
        out_specs=(
            P(("grp", "dev")),
            P(("grp", "dev"), None),
            P(("grp", "dev"), None),
            P("dev", None),
        ),
        check_vma=False,
    )
```

time: 129 us -> 50.5 us (0.39)
  blocking collectives: 47.3 us -> 0 us
  waiting for transfers between devices: 42.4 us -> 15.5 us
  starting transfers between devices: 0.08 us -> 16 us
  between operations: 15.6 us -> 0.76 us
  Pallas kernels: 0 us -> 10.8 us
  local copies, waits for them, and re-layouts: 11.6 us -> 3.69 us
  matrix products: 4.02 us -> 0 us
  other arithmetic: 6.94 us -> 3.48 us
    psum x1 -> x0, waiting for transfers between devices: 41.9 us -> none  [local(): negative_grad = lax.psum(negative_part, 'grp')]
    pmax x1 -> x0, blocking collectives: 17 us -> none  [log_total(): row_max = lax.pmax(maxima, 'dev')]
    all_gather x1 -> x0, blocking collectives: 16.7 us -> none  [local(): group_q = lax.all_gather(queries, 'dev', axis=0, tiled=True)]
    ppermute x0 -> x14, starting transfers between devices: none -> 16 us  [swap(): return lax.ppermute(x, axis, [(i, i ^ mask) for i in range(count)])]
    ppermute x0 -> x14, waiting for transfers between devices: none -> 15.5 us  [swap(): return lax.ppermute(x, axis, [(i, i ^ mask) for i in range(count)])]
    psum x1 -> x0, blocking collectives: 13.6 us -> none  [log_total(): row_sum = lax.psum(totals * jnp.exp(maxima - row_max), 'dev')]
    pallas_call x0 -> x3, Pallas kernels: none -> 10.8 us  [the longest x1 4.21 us: local(): pl.pallas_call(lambda *r: forward_kernel(n, *r), name='fwd', out_shape=[s...]
    dot_general x8 -> x0, matrix products: 4.02 us -> none  [the longest x4 2.24 us: logits(): jnp.dot(q_block, candidates.T, preferred_element_type=jnp.float32)]
  transfers between devices with their start and end apart: 2 -> 14, of which waited for: 1 -> 9; matrix products, arithmetic and copies ran while one was open for 1% -> 8% of each run, Pallas kernels for 0% -> 7%
where the time goes in v1:
time: 50.5 us; the launch traced here: 50.2 us
  starting transfers between devices  16 us (32%)
  waiting for transfers between devices  15.5 us (31%)
  Pallas kernels  10.8 us (21%)
  local copies, waits for them, and re-layouts  3.69 us (7%)
  other arithmetic  3.48 us (7%)
  between operations  0.76 us (2%)
    ppermute x14, starting transfers between devices, swap(): return lax.ppermute(x, axis, [(i, i ^ mask) for i in range(count)])  16 us
    ppermute x14, waiting for transfers between devices, swap(): return lax.ppermute(x, axis, [(i, i ^ mask) for i in range(count)])  15.5 us
    pallas_call x1, Pallas kernels, local(): pl.pallas_call(lambda *r: forward_kernel(n, *r), name='fwd', out_shape=[s...  4.21 us
    pallas_call x1, Pallas kernels, local(): pl.pallas_call(lambda *r: own_kernel(n, *r), name='own', out_shape=[shape...  3.39 us
    pallas_call x1, Pallas kernels, local(): pl.pallas_call(lambda *r: partner_kernel(n, *r), name='partner', out_shap...  3.21 us
    gather x1, local copies, waits for them, and re-layouts, local(): logq_table.at[pair_ids].get(mode='promise_in_bounds').reshape(2, rows)  1.72 us
    unnamed x24, local copies, waits for them, and re-layouts  1.36 us
    another operation x1, other arithmetic  1.1 us
  transfers between devices with their start and end apart: 14, of which 9 were waited for; matrix products, arithmetic and copies ran while one was open for 8% of the time, Pallas kernels for 7%

profile of v1, /device:TPU:0, one launch (start us, length us, event | category | flops | bytes accessed | tf_op | source)
XLA Modules:
  0.0 50.2 jit_solution(4197615186027189320)
XLA Ops:
  0.6 5.1 %collective-permute-start.2 = (bf16[128,256]{1,0:T(8,128)(2,1)}, bf16[128,256]{1,0:T(8,128)(2,1)S(1)}, u32[]{:S(2)}, u32[]{:S(2)}) collective-permute-start(bf16[128,256]{1,0:T(8,128)(2,1)} %r_0_.5), channel_id=1, source_target_pairs={{0,6},{1,7},{2,4},{3,5},{4,2},{5,3},{6,0},{7,1},{8,14},{9,15},{10,... | collective-permute-start | bytes 196616 | tf_op jit(solution)/shard_map/ppermute | solution.py:19
  5.8 0.6 %collective-permute-start = (bf16[128,256]{1,0:T(8,128)(2,1)}, bf16[128,256]{1,0:T(8,128)(2,1)S(1)}, u32[]{:S(2)}, u32[]{:S(2)}) collective-permute-start(bf16[128,256]{1,0:T(8,128)(2,1)} %r_0_.5), channel_id=1, source_target_pairs={{0,2},{1,3},{2,0},{3,1},{4,6},{5,7},{6,4},{7,5},{8,10},{9,11},{10,... | collective-permute-start | bytes 196616 | tf_op jit(solution)/shard_map/ppermute | solution.py:19
  6.4 0.5 %collective-permute-start.4 = (bf16[512,256]{1,0:T(8,128)(2,1)}, bf16[512,256]{1,0:T(8,128)(2,1)S(1)}, u32[]{:S(2)}, u32[]{:S(2)}) collective-permute-start(bf16[512,256]{1,0:T(8,128)(2,1)} %r_5_.1), channel_id=1, source_target_pairs={{0,1},{1,0},{2,3},{3,2},{4,5},{5,4},{6,7},{7,6},{8,9},{9,8},{10,11... | collective-permute-start | bytes 786440 | tf_op jit(solution)/shard_map/ppermute | solution.py:19
  6.9 0.8 %compare_select_fusion = s32[256]{0:T(256)S(1)} fusion(s32[1024]{0:T(1024)} %param.8, s32[]{:T(128)S(6)} %select_n.24), kind=kLoop, calls=%fused_computation.9 | loop fusion | flops 768 | bytes 2052 | tf_op jit(solution)/shard_map/select_n | solution.py:208
  7.7 1.7 %gather_fusion = f32[256]{0:T(256)S(1)} fusion(f32[262144]{0:T(1024)S(1)} %copy-done, s32[1024]{0:T(1024)S(1)} %pad_clamp_fusion), kind=kCustom, calls=%fused_computation | custom fusion | bytes 3072 | tf_op jit(solution)/shard_map/gather | solution.py:208
  9.5 0.1 collective-permute-start.3
  9.6 0.6 %constant_dynamic-slice_fusion = (f32[1,128]{1,0:T(1,128)}, f32[1,128]{1,0:T(1,128)}) fusion(f32[2,128]{1,0:T(2,128)S(1)} %bitcast.4, s32[]{:T(128)S(6)} %select_n.28, s32[]{:T(128)S(6)} %select_n.27), kind=kLoop, calls=%fused_computation.10 | loop fusion | bytes 2056 | tf_op jit(solution)/shard_map/dynamic_slice | solution.py:211
  10.2 0.6 %collective-permute-done.3.r_5_.r_4_ = bf16[128,256]{1,0:T(8,128)(2,1)S(1)} collective-permute-done((bf16[128,256]{1,0:T(8,128)(2,1)S(1)}, bf16[128,256]{1,0:T(8,128)(2,1)S(1)}, u32[]{:S(2)}, u32[]{:S(2)}) %collective-permute-start.3) | collective-permute-done | bytes 65568 | tf_op jit(solution)/shard_map/ppermute | solution.py:19
  10.8 0.8 %collective-permute-done.1.r_2_ = bf16[128,256]{1,0:T(8,128)(2,1)S(1)} collective-permute-done((bf16[128,256]{1,0:T(8,128)(2,1)}, bf16[128,256]{1,0:T(8,128)(2,1)S(1)}, u32[]{:S(2)}, u32[]{:S(2)}) %collective-permute-start.1) | collective-permute-done | bytes 65568 | tf_op jit(solution)/shard_map/ppermute | solution.py:19
  11.7 0.6 %copy-done.8 = bf16[128,256]{1,0:T(8,128)(2,1)} copy-done((bf16[128,256]{1,0:T(8,128)(2,1)}, bf16[128,256]{1,0:T(8,128)(2,1)S(1)}, u32[]{:S(2)}) %copy-start.8) | copy-done | bytes 65560
  12.3 0.1 copy-done.2
  12.4 4.2 %fwd.1 = (f32[256,128]{1,0:T(8,128)}, f32[4,128]{1,0:T(4,128)}, bf16[272,128]{1,0:T(8,128)(2,1)}, bf16[272,128]{1,0:T(8,128)(2,1)}, bf16[272,128]{1,0:T(8,128)(2,1)}) custom-call(bf16[128,256]{1,0:T(8,128)(2,1)} %r_0_.5, bf16[128,256]{1,0:T(8,128)(2,1)} %copy-done.9, bf16[128,256]{1,0:T(8,128)(2,1)} %copy-done.8, bf16[128,256]{1,0:T(8,128)(2,1)} %copy-done.7, ...), custom_call_target="tpu_custom_call" | custom-call | flops 671088640 | bytes 1310720 | tf_op jit(solution)/shard_map/fwd/pallas_call | solution.py:221
  16.6 1.1 %collective-permute-start.6 = (bf16[272,128]{1,0:T(8,128)(2,1)}, bf16[272,128]{1,0:T(8,128)(2,1)S(1)}, u32[]{:S(2)}, u32[]{:S(2)}) collective-permute-start(bf16[272,128]{1,0:T(8,128)(2,1)} %get-tuple-element.15), channel_id=1, source_target_pairs={{0,2},{1,3},{2,0},{3,1},{4,6},{5,7},{6,4},{7,5},{8,10},{9,11},{10,... | collective-permute-start | bytes 208904 | tf_op jit(solution)/shard_map/ppermute | solution.py:19
  17.6 2.5 %collective-permute-start.7 = (bf16[272,128]{1,0:T(8,128)(2,1)}, bf16[272,128]{1,0:T(8,128)(2,1)S(1)}, u32[]{:S(2)}, u32[]{:S(2)}) collective-permute-start(bf16[272,128]{1,0:T(8,128)(2,1)} %get-tuple-element.16), channel_id=1, source_target_pairs={{0,4},{1,5},{2,6},{3,7},{4,0},{5,1},{6,2},{7,3},{8,12},{9,13},{10,... | collective-permute-start | bytes 208904 | tf_op jit(solution)/shard_map/ppermute | solution.py:19
  20.1 0.8 %collective-permute-start.8 = (bf16[272,128]{1,0:T(8,128)(2,1)}, bf16[272,128]{1,0:T(8,128)(2,1)S(1)}, u32[]{:S(2)}, u32[]{:S(2)}) collective-permute-start(bf16[272,128]{1,0:T(8,128)(2,1)} %get-tuple-element.17), channel_id=1, source_target_pairs={{0,6},{1,7},{2,4},{3,5},{4,2},{5,3},{6,0},{7,1},{8,14},{9,15},{10,... | collective-permute-start | bytes 208904 | tf_op jit(solution)/shard_map/ppermute | solution.py:19
  20.9 0.1 collective-permute-done.6.r_10_.r_9_
  21.1 4.6 %collective-permute-done.7.r_11_.r_10_ = bf16[272,128]{1,0:T(8,128)(2,1)S(1)} collective-permute-done((bf16[272,128]{1,0:T(8,128)(2,1)}, bf16[272,128]{1,0:T(8,128)(2,1)S(1)}, u32[]{:S(2)}, u32[]{:S(2)}) %collective-permute-start.7) | collective-permute-done | bytes 69664 | tf_op jit(solution)/shard_map/ppermute | solution.py:19
  25.7 0.8 %collective-permute-done.8.r_12_.r_11_ = bf16[272,128]{1,0:T(8,128)(2,1)S(1)} collective-permute-done((bf16[272,128]{1,0:T(8,128)(2,1)}, bf16[272,128]{1,0:T(8,128)(2,1)S(1)}, u32[]{:S(2)}, u32[]{:S(2)}) %collective-permute-start.8) | collective-permute-done | bytes 69664 | tf_op jit(solution)/shard_map/ppermute | solution.py:19
  26.5 0.6 %copy-done.5 = bf16[272,128]{1,0:T(8,128)(2,1)} copy-done((bf16[272,128]{1,0:T(8,128)(2,1)}, bf16[272,128]{1,0:T(8,128)(2,1)S(1)}, u32[]{:S(2)}) %copy-start.5) | copy-done | bytes 69656
  27.2 3.2 %partner.1 = bf16[640,256]{1,0:T(8,128)(2,1)} custom-call(bf16[128,256]{1,0:T(8,128)(2,1)} %r_0_.5, bf16[128,256]{1,0:T(8,128)(2,1)} %copy-done.9, bf16[128,256]{1,0:T(8,128)(2,1)} %copy-done.8, bf16[128,256]{1,0:T(8,128)(2,1)} %copy-done.7, bf16[128,256]{1,0:T(8,128)(2,1)} %copy-done.10, bf16[512,256]{1,0:T(8,128)(2,1)} %copy-done.2, ...), custom_call_target="tpu_custom_call" | custom-call | flops 335544320 | bytes 1310720 | tf_op jit(solution)/shard_map/partner/pallas_call | solution.py:248
  30.4 3.4 %own.1 = (f32[1,128]{1,0:T(1,128)}, f32[128,256]{1,0:T(8,128)}, f32[128,256]{1,0:T(8,128)}, f32[512,256]{1,0:T(8,128)}) custom-call(bf16[128,256]{1,0:T(8,128)(2,1)} %r_0_.5, bf16[128,256]{1,0:T(8,128)(2,1)} %copy-done.9, bf16[128,256]{1,0:T(8,128)(2,1)} %copy-done.8, bf16[128,256]{1,0:T(8,128)(2,1)} %copy-done.7, bf16[128,256]{1,0:T(8,128)(2,1)} %r_4_.3, ...), custom_call_target="tpu_custom_call" | custom-call | flops 335544320 | bytes 1310720 | tf_op jit(solution)/shard_map/own/pallas_call | solution.py:258
  33.8 1.1 %add_convert_fusion = bf16[512,256]{1,0:T(8,128)(2,1)S(1)} fusion(f32[512,256]{1,0:T(8,128)} %get-tuple-element.21, bf16[640,256]{1,0:T(8,128)(2,1)S(1)} %collective-permute-done.9), kind=kLoop, calls=%fused_computation.2 | loop fusion | flops 393216 | bytes 1048576 | tf_op jit(solution)/shard_map/convert.1
  34.9 1.6 %collective-permute-start.10 = (bf16[256,256]{1,0:T(8,128)(2,1)S(1)}, bf16[256,256]{1,0:T(8,128)(2,1)S(1)}, u32[]{:S(2)}, u32[]{:S(2)}) collective-permute-start(bf16[256,256]{1,0:T(8,128)(2,1)S(1)} %get-tuple-element.24), channel_id=1, source_target_pairs={{0,8},{8,0},{16,24},{24,16},{1,9},{9,1},{17,25},{25,17},{2,10},{10... | collective-permute-start | bytes 393224 | tf_op jit(solution)/shard_map/ppermute | solution.py:19
  36.5 1.5 %collective-permute-start.12 = (bf16[256,256]{1,0:T(8,128)(2,1)S(1)}, bf16[256,256]{1,0:T(8,128)(2,1)S(1)}, u32[]{:S(2)}, u32[]{:S(2)}) collective-permute-start(bf16[256,256]{1,0:T(8,128)(2,1)S(1)} %get-tuple-element.25), channel_id=1, source_target_pairs={{0,16},{8,24},{16,0},{24,8},{1,17},{9,25},{17,1},{25,9},{2,18},{10... | collective-permute-start | bytes 393224 | tf_op jit(solution)/shard_map/ppermute | solution.py:19
  38.0 2.9 %collective-permute-done.10 = bf16[256,256]{1,0:T(8,128)(2,1)S(1)} collective-permute-done((bf16[256,256]{1,0:T(8,128)(2,1)S(1)}, bf16[256,256]{1,0:T(8,128)(2,1)S(1)}, u32[]{:S(2)}, u32[]{:S(2)}) %collective-permute-start.10) | collective-permute-done | bytes 131104 | tf_op jit(solution)/shard_map/ppermute | solution.py:19
  40.9 1.2 %collective-permute-done.12 = bf16[256,256]{1,0:T(8,128)(2,1)S(1)} collective-permute-done((bf16[256,256]{1,0:T(8,128)(2,1)S(1)}, bf16[256,256]{1,0:T(8,128)(2,1)S(1)}, u32[]{:S(2)}, u32[]{:S(2)}) %collective-permute-start.12) | collective-permute-done | bytes 131104 | tf_op jit(solution)/shard_map/ppermute | solution.py:19
  42.2 1.6 %collective-permute-start.11 = (bf16[256,256]{1,0:T(8,128)(2,1)S(1)}, bf16[256,256]{1,0:T(8,128)(2,1)S(1)}, u32[]{:S(2)}, u32[]{:S(2)}) collective-permute-start(bf16[256,256]{1,0:T(8,128)(2,1)S(1)} %get-tuple-element.22), channel_id=1, source_target_pairs={{0,16},{8,24},{16,0},{24,8},{1,17},{9,25},{17,1},{25,9},{2,18},{10... | collective-permute-start | bytes 393224 | tf_op jit(solution)/shard_map/ppermute | solution.py:19
  43.7 0.7 %convert_add_fusion.2 = f32[128,256]{1,0:T(8,128)} fusion(f32[128,256]{1,0:T(8,128)S(1)} %copy-done.1, bf16[640,256]{1,0:T(8,128)(2,1)S(1)} %collective-permute-done.9), kind=kLoop, calls=%fused_computation.7 | loop fusion | flops 65536 | bytes 327680 | tf_op jit(solution)/shard_map/add | solution.py:273
  44.4 0.5 %collective-permute-start.13 = (bf16[256,256]{1,0:T(8,128)(2,1)S(1)}, bf16[256,256]{1,0:T(8,128)(2,1)S(1)}, u32[]{:S(2)}, u32[]{:S(2)}) collective-permute-start(bf16[256,256]{1,0:T(8,128)(2,1)S(1)} %get-tuple-element.23), channel_id=1, source_target_pairs={{0,8},{8,0},{16,24},{24,16},{1,9},{9,1},{17,25},{25,17},{2,10},{10... | collective-permute-start | bytes 393224 | tf_op jit(solution)/shard_map/ppermute | solution.py:19
  44.9 2.2 %collective-permute-done.11 = bf16[256,256]{1,0:T(8,128)(2,1)S(1)} collective-permute-done((bf16[256,256]{1,0:T(8,128)(2,1)S(1)}, bf16[256,256]{1,0:T(8,128)(2,1)S(1)}, u32[]{:S(2)}, u32[]{:S(2)}) %collective-permute-start.11) | collective-permute-done | bytes 131104 | tf_op jit(solution)/shard_map/ppermute | solution.py:19
  47.2 2.2 %collective-permute-done.13 = bf16[256,256]{1,0:T(8,128)(2,1)S(1)} collective-permute-done((bf16[256,256]{1,0:T(8,128)(2,1)S(1)}, bf16[256,256]{1,0:T(8,128)(2,1)S(1)}, u32[]{:S(2)}, u32[]{:S(2)}) %collective-permute-start.13) | collective-permute-done | bytes 131104 | tf_op jit(solution)/shard_map/ppermute | solution.py:19
  49.4 0.8 %pad_maximum_fusion = f32[512,256]{1,0:T(8,128)} fusion(f32[256,256]{1,0:T(8,128)S(1)} %convert_add_fusion, f32[256,256]{1,0:T(8,128)S(1)} %convert_add_fusion.1), kind=kLoop, calls=%fused_computation.1 | loop fusion | flops 131072 | bytes 1048576 | tf_op jit(solution)/shard_map/concatenate | solution.py:286
  (34 shorter events, 0.3 us)
Async XLA Ops:
  0.6 7.1 %copy-start = (f32[262144]{0:T(1024)S(1)}, f32[262144]{0:T(1024)}, u32[]{:S(2)}) copy-start(f32[262144]{0:T(1024)} %param.11) | copy-start | bytes 3145732
  0.6 10.2 %collective-permute-start.2 = (bf16[128,256]{1,0:T(8,128)(2,1)}, bf16[128,256]{1,0:T(8,128)(2,1)S(1)}, u32[]{:S(2)}, u32[]{:S(2)}) collective-permute-start(bf16[128,256]{1,0:T(8,128)(2,1)} %r_0_.5), channel_id=1, source_target_pairs={{0,6},{1,7},{2,4},{3,5},{4,2},{5,3},{6,0},{7,1},{8,14},{9,15},{10,... | collective-permute-start | bytes 196616 | tf_op jit(solution)/shard_map/ppermute | solution.py:19
  5.8 5.8 %collective-permute-start.1 = (bf16[128,256]{1,0:T(8,128)(2,1)}, bf16[128,256]{1,0:T(8,128)(2,1)S(1)}, u32[]{:S(2)}, u32[]{:S(2)}) collective-permute-start(bf16[128,256]{1,0:T(8,128)(2,1)} %r_0_.5), channel_id=1, source_target_pairs={{0,4},{1,5},{2,6},{3,7},{4,0},{5,1},{6,2},{7,3},{8,12},{9,13},{10,... | collective-permute-start | bytes 196616 | tf_op jit(solution)/shard_map/ppermute | solution.py:19
  5.8 5.8 %collective-permute-start = (bf16[128,256]{1,0:T(8,128)(2,1)}, bf16[128,256]{1,0:T(8,128)(2,1)S(1)}, u32[]{:S(2)}, u32[]{:S(2)}) collective-permute-start(bf16[128,256]{1,0:T(8,128)(2,1)} %r_0_.5), channel_id=1, source_target_pairs={{0,2},{1,3},{2,0},{3,1},{4,6},{5,7},{6,4},{7,5},{8,10},{9,11},{10,... | collective-permute-start | bytes 196616 | tf_op jit(solution)/shard_map/ppermute | solution.py:19
  6.4 3.0 %collective-permute-start.5 = (f32[512]{0:T(512)}, f32[512]{0:T(512)S(1)}, u32[]{:S(2)}, u32[]{:S(2)}) collective-permute-start(f32[512]{0:T(512)} %param.10), channel_id=1, source_target_pairs={{0,1},{1,0},{2,3},{3,2},{4,5},{5,4},{6,7},{7,6},{8,9},{9,8},{10,11... | collective-permute-start | bytes 6152 | tf_op jit(solution)/shard_map/ppermute | solution.py:19
  6.4 5.2 %collective-permute-start.4 = (bf16[512,256]{1,0:T(8,128)(2,1)}, bf16[512,256]{1,0:T(8,128)(2,1)S(1)}, u32[]{:S(2)}, u32[]{:S(2)}) collective-permute-start(bf16[512,256]{1,0:T(8,128)(2,1)} %r_5_.1), channel_id=1, source_target_pairs={{0,1},{1,0},{2,3},{3,2},{4,5},{5,4},{6,7},{7,6},{8,9},{9,8},{10,11... | collective-permute-start | bytes 786440 | tf_op jit(solution)/shard_map/ppermute | solution.py:19
  7.7 1.8 %copy-start.6 = (bf16[128,256]{1,0:T(8,128)(2,1)S(1)}, bf16[128,256]{1,0:T(8,128)(2,1)}, u32[]{:S(2)}) copy-start(bf16[128,256]{1,0:T(8,128)(2,1)} %r_4_.3) | copy-start | bytes 196612
  9.5 0.7 %copy-start.11 = (f32[512]{0:T(512)}, f32[512]{0:T(512)S(1)}, u32[]{:S(2)}) copy-start(f32[512]{0:T(512)S(1)} %collective-permute-done.5) | copy-start | bytes 6148
  9.5 1.3 %collective-permute-start.3 = (bf16[128,256]{1,0:T(8,128)(2,1)S(1)}, bf16[128,256]{1,0:T(8,128)(2,1)S(1)}, u32[]{:S(2)}, u32[]{:S(2)}) collective-permute-start(bf16[128,256]{1,0:T(8,128)(2,1)S(1)} %copy-done.6), channel_id=1, source_target_pairs={{0,1},{1,0},{2,3},{3,2},{4,5},{5,4},{6,7},{7,6},{8,9},{9,8},{10,11... | collective-permute-start | bytes 196616 | tf_op jit(solution)/shard_map/ppermute | solution.py:19
  10.8 0.8 %copy-start.10 = (bf16[128,256]{1,0:T(8,128)(2,1)}, bf16[128,256]{1,0:T(8,128)(2,1)S(1)}, u32[]{:S(2)}) copy-start(bf16[128,256]{1,0:T(8,128)(2,1)S(1)} %collective-permute-done.3.r_5_.r_4_) | copy-start | bytes 196612
  10.8 0.8 %copy-start.7 = (bf16[128,256]{1,0:T(8,128)(2,1)}, bf16[128,256]{1,0:T(8,128)(2,1)S(1)}, u32[]{:S(2)}) copy-start(bf16[128,256]{1,0:T(8,128)(2,1)S(1)} %collective-permute-done.2.r_3_) | copy-start | bytes 196612
  11.6 0.6 %copy-start.8 = (bf16[128,256]{1,0:T(8,128)(2,1)}, bf16[128,256]{1,0:T(8,128)(2,1)S(1)}, u32[]{:S(2)}) copy-start(bf16[128,256]{1,0:T(8,128)(2,1)S(1)} %collective-permute-done.1.r_2_) | copy-start | bytes 196612
  11.6 0.7 %copy-start.9 = (bf16[128,256]{1,0:T(8,128)(2,1)}, bf16[128,256]{1,0:T(8,128)(2,1)S(1)}, u32[]{:S(2)}) copy-start(bf16[128,256]{1,0:T(8,128)(2,1)S(1)} %collective-permute-done.r_1_) | copy-start | bytes 196612
  11.6 0.7 %copy-start.2 = (bf16[512,256]{1,0:T(8,128)(2,1)}, bf16[512,256]{1,0:T(8,128)(2,1)S(1)}, u32[]{:S(2)}) copy-start(bf16[512,256]{1,0:T(8,128)(2,1)S(1)} %collective-permute-done.4.r_7_.r_5_) | copy-start | bytes 786436
  16.6 4.5 %collective-permute-start.6 = (bf16[272,128]{1,0:T(8,128)(2,1)}, bf16[272,128]{1,0:T(8,128)(2,1)S(1)}, u32[]{:S(2)}, u32[]{:S(2)}) collective-permute-start(bf16[272,128]{1,0:T(8,128)(2,1)} %get-tuple-element.15), channel_id=1, source_target_pairs={{0,2},{1,3},{2,0},{3,1},{4,6},{5,7},{6,4},{7,5},{8,10},{9,11},{10,... | collective-permute-start | bytes 208904 | tf_op jit(solution)/shard_map/ppermute | solution.py:19
  17.6 8.1 %collective-permute-start.7 = (bf16[272,128]{1,0:T(8,128)(2,1)}, bf16[272,128]{1,0:T(8,128)(2,1)S(1)}, u32[]{:S(2)}, u32[]{:S(2)}) collective-permute-start(bf16[272,128]{1,0:T(8,128)(2,1)} %get-tuple-element.16), channel_id=1, source_target_pairs={{0,4},{1,5},{2,6},{3,7},{4,0},{5,1},{6,2},{7,3},{8,12},{9,13},{10,... | collective-permute-start | bytes 208904 | tf_op jit(solution)/shard_map/ppermute | solution.py:19
  20.1 6.4 %collective-permute-start.8 = (bf16[272,128]{1,0:T(8,128)(2,1)}, bf16[272,128]{1,0:T(8,128)(2,1)S(1)}, u32[]{:S(2)}, u32[]{:S(2)}) collective-permute-start(bf16[272,128]{1,0:T(8,128)(2,1)} %get-tuple-element.17), channel_id=1, source_target_pairs={{0,6},{1,7},{2,4},{3,5},{4,2},{5,3},{6,0},{7,1},{8,14},{9,15},{10,... | collective-permute-start | bytes 208904 | tf_op jit(solution)/shard_map/ppermute | solution.py:19
  21.1 5.4 %copy-start.3 = (bf16[272,128]{1,0:T(8,128)(2,1)}, bf16[272,128]{1,0:T(8,128)(2,1)S(1)}, u32[]{:S(2)}) copy-start(bf16[272,128]{1,0:T(8,128)(2,1)S(1)} %collective-permute-done.6.r_10_.r_9_) | copy-start | bytes 208900
  25.7 0.8 %copy-start.4 = (bf16[272,128]{1,0:T(8,128)(2,1)}, bf16[272,128]{1,0:T(8,128)(2,1)S(1)}, u32[]{:S(2)}) copy-start(bf16[272,128]{1,0:T(8,128)(2,1)S(1)} %collective-permute-done.7.r_11_.r_10_) | copy-start | bytes 208900
  26.5 0.6 %copy-start.5 = (bf16[272,128]{1,0:T(8,128)(2,1)}, bf16[272,128]{1,0:T(8,128)(2,1)S(1)}, u32[]{:S(2)}) copy-start(bf16[272,128]{1,0:T(8,128)(2,1)S(1)} %collective-permute-done.8.r_12_.r_11_) | copy-start | bytes 208900
  30.4 3.4 %collective-permute-start.9 = (bf16[640,256]{1,0:T(8,128)(2,1)}, bf16[640,256]{1,0:T(8,128)(2,1)S(1)}, u32[]{:S(2)}, u32[]{:S(2)}) collective-permute-start(bf16[640,256]{1,0:T(8,128)(2,1)} %partner.1), channel_id=1, source_target_pairs={{0,1},{1,0},{2,3},{3,2},{4,5},{5,4},{6,7},{7,6},{8,9},{9,8},{10,11... | collective-permute-start | bytes 983048 | tf_op jit(solution)/shard_map/ppermute | solution.py:19
  34.9 6.0 %collective-permute-start.10 = (bf16[256,256]{1,0:T(8,128)(2,1)S(1)}, bf16[256,256]{1,0:T(8,128)(2,1)S(1)}, u32[]{:S(2)}, u32[]{:S(2)}) collective-permute-start(bf16[256,256]{1,0:T(8,128)(2,1)S(1)} %get-tuple-element.24), channel_id=1, source_target_pairs={{0,8},{8,0},{16,24},{24,16},{1,9},{9,1},{17,25},{25,17},{2,10},{10... | collective-permute-start | bytes 393224 | tf_op jit(solution)/shard_map/ppermute | solution.py:19
  36.4 7.3 %copy-start.1 = (f32[128,256]{1,0:T(8,128)S(1)}, f32[128,256]{1,0:T(8,128)}, u32[]{:S(2)}) copy-start(f32[128,256]{1,0:T(8,128)} %get-tuple-element.20) | copy-start | bytes 393220
  36.5 5.6 %collective-permute-start.12 = (bf16[256,256]{1,0:T(8,128)(2,1)S(1)}, bf16[256,256]{1,0:T(8,128)(2,1)S(1)}, u32[]{:S(2)}, u32[]{:S(2)}) collective-permute-start(bf16[256,256]{1,0:T(8,128)(2,1)S(1)} %get-tuple-element.25), channel_id=1, source_target_pairs={{0,16},{8,24},{16,0},{24,8},{1,17},{9,25},{17,1},{25,9},{2,18},{10... | collective-permute-start | bytes 393224 | tf_op jit(solution)/shard_map/ppermute | solution.py:19
  42.2 5.0 %collective-permute-start.11 = (bf16[256,256]{1,0:T(8,128)(2,1)S(1)}, bf16[256,256]{1,0:T(8,128)(2,1)S(1)}, u32[]{:S(2)}, u32[]{:S(2)}) collective-permute-start(bf16[256,256]{1,0:T(8,128)(2,1)S(1)} %get-tuple-element.22), channel_id=1, source_target_pairs={{0,16},{8,24},{16,0},{24,8},{1,17},{9,25},{17,1},{25,9},{2,18},{10... | collective-permute-start | bytes 393224 | tf_op jit(solution)/shard_map/ppermute | solution.py:19
  44.4 5.0 %collective-permute-start.13 = (bf16[256,256]{1,0:T(8,128)(2,1)S(1)}, bf16[256,256]{1,0:T(8,128)(2,1)S(1)}, u32[]{:S(2)}, u32[]{:S(2)}) collective-permute-start(bf16[256,256]{1,0:T(8,128)(2,1)S(1)} %get-tuple-element.23), channel_id=1, source_target_pairs={{0,8},{8,0},{16,24},{24,16},{1,9},{9,1},{17,25},{25,17},{2,10},{10... | collective-permute-start | bytes 393224 | tf_op jit(solution)/shard_map/ppermute | solution.py:19

commit v2 on v0

v2 whole, which is shorter than its diff:
```python
import jax
import jax.numpy as jnp
from jax import lax
from jax.experimental import pallas as pl
from jax.experimental.pallas import tpu as pltpu
from jax.sharding import PartitionSpec as P

logit_scale = 0.25
LANES = 128
F32, BF16 = jnp.float32, jnp.bfloat16
NT = (((1,), (1,)), ((), ()))
GRANT = 16 << 20


def round_up(x, m):
    return -(-x // m) * m


def swap(x, axis, count, mask):
    return lax.ppermute(x, axis, [(i, i ^ mask) for i in range(count)])


def fold(x, op):
    rows, cols = x.shape
    return op(x.reshape(rows // 8, 8, cols), axis=0)


def pad_rows(parts, multiple):
    have = sum(p.shape[0] for p in parts)
    lack = round_up(have, multiple) - have
    if lack:
        parts = parts + [jnp.zeros((lack, parts[0].shape[1]), parts[0].dtype)]
    return jnp.concatenate(parts, axis=0)


def split3(x):
    hi = x.astype(BF16)
    rest = x - hi.astype(F32)
    mid = rest.astype(BF16)
    return [hi, mid, (rest - mid.astype(F32)).astype(BF16)]


def runs_of(refs, rows):
    return [(ref, first) for ref in refs for first in range(0, ref.shape[0], rows)]


def scores(ref, first, rows, q, col):
    s = lax.dot_general(ref[first : first + rows, :], q, NT, preferred_element_type=F32)
    return logit_scale * s - col


def log_total(runs, cols_ref, q, s_all):
    rows = q.shape[0]
    top = None
    for j, (ref, first) in enumerate(runs):
        s = scores(ref, first, rows, q, cols_ref[:, j : j + 1])
        s_all[j * rows : (j + 1) * rows, :] = s
        here = fold(s, jnp.max)
        top = here if top is None else jnp.maximum(top, here)
    row_max = jnp.max(top, axis=0, keepdims=True)
    total = None
    for j in range(len(runs)):
        here = fold(jnp.exp(s_all[j * rows : (j + 1) * rows, :] - row_max), jnp.sum)
        total = here if total is None else total + here
    return row_max + jnp.log(jnp.sum(total, axis=0, keepdims=True))


def own_block_kernel(ids_ref, table_ref, q_ref, *refs):
    (it_o, neg_o, lq_o, it_p, neg_p, lq_p), refs = refs[:6], refs[6:]
    lse_ref, cols_ref, ct_ref, q_copy, it_copy, neg_copy, picked, s_all = refs
    c_refs = (it_o, it_p, neg_o, neg_p)
    rows, _ = q_ref.shape
    q_copy[...] = q_ref[...]
    it_copy[...] = it_o[...]
    neg_copy[...] = neg_o[...]
    dev = lax.axis_index("dev")
    lane = lax.broadcasted_iota(jnp.int32, (1, LANES), 1)
    for half, owner in enumerate((dev, dev ^ 1)):
        start = owner * rows

        def pick(i, carry, half=half, start=start):
            for t in range(8):
                j = i * 8 + t
                item = ids_ref[start + j]
                row = table_ref[pl.ds(lax.shift_right_logical(item, 7), 1), :]
                picked[pl.ds(half * rows + j, 1), :] = jnp.where(lane == (item & (LANES - 1)), row, 0.0)
            return carry

        lax.fori_loop(0, rows // 8, pick, 0)
    for half in range(2):
        part = picked[half * rows : (half + 1) * rows, :]
        cols_ref[:, half : half + 1] = jnp.sum(part, axis=1, keepdims=True)
    lq = pad_rows([lq_o[...], lq_p[...]], 8).T
    count = lq_o.shape[0] + lq_p.shape[0]
    cols_ref[:, 2 : 2 + count] = lq[:, :count]
    runs = runs_of(c_refs, rows)
    for j, (ref, first) in enumerate(runs):
        ct_ref[:, j * rows : (j + 1) * rows] = ref[first : first + rows, :].T
    lse_ref[...] = log_total(runs, cols_ref, q_ref[...], s_all)


def other_blocks_kernel(n, *refs):
    q_refs, refs = refs[: n - 1], refs[n - 1 :]
    c_refs, (cols_ref, lse0_ref), (lse_ref, msg_ref, s_all) = refs[:4], refs[4:6], refs[6:]
    rows, _ = q_refs[0].shape
    runs = runs_of(c_refs, rows)
    lse_ref[0:1, :] = lse0_ref[...]
    for k in range(1, n):
        lse_ref[k : k + 1, :] = log_total(runs, cols_ref, q_refs[k - 1][...], s_all)
    msg_ref[...] = pad_rows(split3(lse_ref[...]), 16)


def gradient(n, q_all, runs, cols, norm_ref, mask_first, p_ref, emit):
    rows = q_all.shape[0] // n
    per = 2 if n % 2 == 0 else 1
    chunk = per * rows
    matched = None
    for j, (ref, first) in enumerate(runs):
        for p in range(n // per):
            norm = jnp.concatenate([norm_ref[b : b + 1, :] for b in range(p * per, (p + 1) * per)], axis=1)
            q = q_all[p * chunk : (p + 1) * chunk, :]
            s = scores(ref, first, rows, q, cols[j]) if per == 1 else (
                logit_scale
                * lax.dot_general(ref[first : first + rows, :], q, NT, preferred_element_type=F32)
                - cols[j]
            )
            prob = jnp.exp(s - norm)
            if mask_first and j == 0 and p == 0:
                hit = lax.broadcasted_iota(jnp.int32, s.shape, 0) == lax.broadcasted_iota(
                    jnp.int32, s.shape, 1
                )
                matched = jnp.sum(jnp.where(hit, s, 0.0), axis=0, keepdims=True)[:, :rows]
                prob = prob - hit.astype(F32)
            p_ref[j * rows : (j + 1) * rows, p * chunk : (p + 1) * chunk] = (logit_scale * prob).astype(BF16)
        emit(j, jnp.dot(p_ref[j * rows : (j + 1) * rows, :], q_all[...], preferred_element_type=F32))
    return matched


def partner_kernel(n, first_col, *refs):
    q_refs, refs = refs[:n], refs[n:]
    neg_ref, cols_ref, lse_ref, refs = refs[0], refs[1], refs[2], refs[3:]
    got_refs, (out_ref, p_ref, norm_ref, q_all) = refs[: n - 1], refs[n - 1 :]
    rows, _ = q_refs[0].shape
    for k in range(n):
        q_all[k * rows : (k + 1) * rows, :] = q_refs[k][...]
    totals = [lse_ref[...]]
    for ref in got_refs:
        got = ref[...].astype(F32)
        totals.append(got[:n] + got[n : 2 * n] + got[2 * n : 3 * n])
    for b in range(n):
        parts = [totals[k][k ^ b : (k ^ b) + 1, :] for k in range(n)]
        top = parts[0]
        for r in parts[1:]:
            top = jnp.maximum(top, r)
        total = jnp.exp(parts[0] - top)
        for r in parts[1:]:
            total = total + jnp.exp(r - top)
        norm_ref[b : b + 1, :] = top + jnp.log(total)
    runs = runs_of([neg_ref], rows)
    cols = [cols_ref[:, first_col + j : first_col + j + 1] for j in range(len(runs))]

    def emit(j, g):
        out_ref[j * rows : (j + 1) * rows, :] = g.astype(BF16)

    gradient(n, q_all, runs, cols, norm_ref, False, p_ref, emit)


def own_kernel(n, first_col, q_all, neg_ref, cols_ref, norm_ref, out_ref, p_ref):
    rows = q_all.shape[0] // n
    runs = runs_of([neg_ref], rows)
    cols = [cols_ref[:, first_col + j : first_col + j + 1] for j in range(len(runs))]

    def emit(j, g):
        out_ref[j * rows : (j + 1) * rows, :] = g

    gradient(n, q_all, runs, cols, norm_ref, False, p_ref, emit)


def items_kernel(n, *refs):
    (q_all, it_o, it_p, cols_ref, norm_ref, ct_ref, p_own, p_par), refs = refs[:8], refs[8:]
    (_, loss_ref, mine_ref, theirs_ref, own_ref), refs = refs[:5], refs[5:]
    msg_refs, (p_ref,) = refs[: n - 1], refs[n - 1 :]
    rows = q_all.shape[0] // n
    negs = p_own.shape[0]

    def emit(j, g):
        if j == 0:
            mine_ref[...] = g
        else:
            theirs_ref[...] = g.astype(BF16)

    cols = [cols_ref[:, j : j + 1] for j in range(2)]
    matched = gradient(n, q_all, runs_of([it_o, it_p], rows), cols, norm_ref, True, p_ref, emit)
    loss_ref[...] = norm_ref[0:1, :] - matched
    for k in range(n):
        part = slice(k * rows, (k + 1) * rows)
        u = jnp.dot(ct_ref[:, : 2 * rows], p_ref[:, part], preferred_element_type=F32)
        u += jnp.dot(ct_ref[:, 2 * rows : 2 * rows + negs], p_own[:, part], preferred_element_type=F32)
        u += jnp.dot(ct_ref[:, 2 * rows + negs :], p_par[:, part], preferred_element_type=F32)
        if k == 0:
            own_ref[...] = u
        else:
            msg_refs[k - 1][...] = u.astype(BF16)


def query_kernel(own_ref, *refs):
    total = own_ref[...]
    for ref in refs[:-1]:
        total = total + ref[...].astype(F32)
    refs[-1][...] = total.T


def local_fn(mesh):
    n_dev, n_grp = mesh.shape["dev"], mesh.shape["grp"]
    n = n_dev // 2
    masks = [1 << i for i in range((n_grp - 1).bit_length())]

    def call(kernel, outs, args, scratch=(), cost=None, smem=0, raw=0):
        shapes = [
            jax.ShapeDtypeStruct(o.shape, o.dtype) if isinstance(o, jax.ShapeDtypeStruct) else pltpu.VMEM(*o)
            for o in outs
        ]
        spec = pl.BlockSpec(memory_space=pltpu.VMEM)
        specs = [pl.BlockSpec(memory_space=pltpu.SMEM)] * smem + [spec] * (len(args) - smem)
        args = list(args[:raw]) + [pltpu.with_memory_space_constraint(a, pltpu.VMEM) for a in args[raw:]]
        flops, exps = cost
        return pl.pallas_call(
            kernel,
            out_shape=shapes,
            in_specs=specs,
            out_specs=[spec] * len(outs),
            scratch_shapes=list(scratch),
            cost_estimate=pl.CostEstimate(flops=flops, bytes_accessed=0, transcendentals=exps),
            compiler_params=pltpu.CompilerParams(vmem_limit_bytes=GRANT),
        )(*args)

    def butterfly(x, t):
        steps = len(masks)
        pairs = []
        for g in range(n_grp):
            for d in range(n_dev):
                mask = masks[(t + d % 2) % steps]
                pairs.append((g * n_dev + d, (g ^ mask) * n_dev + d))
        return lax.ppermute(x, ("grp", "dev"), pairs)

    def local(queries, items, item_ids, neg_embed, neg_logq, logq_table):
        return step(queries, items, item_ids, neg_embed, neg_logq, logq_table)

    def exchange(x, k):
        return swap(x, "dev", n_dev, 2 * k)

    def partner(x):
        return swap(x, "dev", n_dev, 1)

    def step(queries, items, item_ids, neg_embed, neg_logq, logq_table):
        rows, width = queries.shape
        negs = neg_embed.shape[0]
        others = [exchange(queries, k) for k in range(1, n)]
        items_p = partner(items)
        neg_p = partner(neg_embed)
        logq_p = partner(neg_logq)
        lq_o = neg_logq.reshape(negs // rows, rows)
        lq_p = logq_p.reshape(negs // rows, rows)
        table = logq_table.reshape(-1, LANES)
        cands = 2 * (rows + negs)
        unit = 2 * rows * width
        shape = jax.ShapeDtypeStruct

        lse0, cols, c_t, q0, items, neg_embed = call(
            own_block_kernel,
            [
                ((1, rows), F32),
                ((rows, LANES), F32),
                ((width, cands), BF16),
                ((rows, width), BF16),
                ((rows, width), BF16),
                ((negs, width), BF16),
            ],
            (item_ids, table, queries, items, neg_embed, lq_o, items_p, neg_p, lq_p),
            [pltpu.VMEM((2 * rows, LANES), F32), pltpu.VMEM((cands, rows), F32)],
            (unit * cands, rows * cands),
            smem=1,
            raw=6,
        )
        q = [q0] + others
        msg_rows = round_up(3 * n, 16)
        lse, msg = call(
            lambda *r: other_blocks_kernel(n, *r),
            [((n, rows), F32), ((msg_rows, rows), BF16)],
            (*others, items, items_p, neg_embed, neg_p, cols, lse0),
            [pltpu.VMEM((cands, rows), F32)],
            ((n - 1) * unit * cands, (n - 1) * rows * cands),
        )
        got = [exchange(msg, k) for k in range(1, n)]
        per_run = negs // rows
        theirs, p_par, norm, q_all = call(
            lambda *r: partner_kernel(n, 2 + per_run, *r),
            [((negs, width), BF16), ((negs, n * rows), BF16), ((n, rows), F32), ((n * rows, width), BF16)],
            (*q, neg_p, cols, lse, *got),
            (),
            (2 * n * unit * negs, n * rows * negs),
        )
        back = partner(theirs)
        mine, p_own = call(
            lambda *r: own_kernel(n, 2, *r),
            [((negs, width), F32), ((negs, n * rows), BF16)],
            (q_all, neg_embed, cols, norm),
            (),
            (2 * n * unit * negs, n * rows * negs),
        )
        part = (mine + back.astype(F32)).astype(BF16)
        loss, item_mine, item_theirs, u_own, *u_msgs = call(
            lambda *r: items_kernel(n, *r),
            [((1, rows), F32), ((rows, width), F32), ((rows, width), BF16), ((width, rows), F32)]
            + [((width, rows), BF16)] * (n - 1),
            (q_all, items, items_p, cols, norm, c_t, p_own, p_par, part),
            [pltpu.VMEM((2 * rows, n * rows), BF16)],
            (3 * n * unit * cands, 2 * n * rows * rows),
        )
        item_back = partner(item_theirs)
        u_got = [exchange(u_msgs[k - 1], k) for k in range(1, n)]
        (query_grad,) = call(query_kernel, [shape((rows, width), F32)], (u_own, *u_got), (), (n * rows * width, 0))
        for t in range(len(masks)):
            other = butterfly(part, t)
            total = part.astype(F32) + other.astype(F32)
            part = total.astype(BF16)
        item_grad = item_mine + item_back.astype(F32)
        return (loss.reshape(rows), query_grad, item_grad, total)

    return local


def solution(mesh):
    return jax.shard_map(
        local_fn(mesh),
        mesh=mesh,
        in_specs=(
            P(("grp", "dev"), None),
            P(("grp", "dev"), None),
            P("grp"),
            P("dev", None),
            P("dev"),
            P(),
        ),
        out_specs=(
            P(("grp", "dev")),
            P(("grp", "dev"), None),
            P(("grp", "dev"), None),
            P("dev", None),
        ),
        check_vma=False,
    )
```

time: 129 us -> 39.8 us (0.31)
  blocking collectives: 47.3 us -> 0 us
  waiting for transfers between devices: 42.4 us -> 6.46 us
  starting transfers between devices: 0.08 us -> 18.4 us
  between operations: 15.6 us -> 0.72 us
  Pallas kernels: 0 us -> 7.24 us
  local copies, waits for them, and re-layouts: 11.6 us -> 5.04 us
  other arithmetic: 6.94 us -> 1.65 us
  matrix products: 4.02 us -> 0 us
    psum x1 -> x0, waiting for transfers between devices: 41.9 us -> none  [local(): negative_grad = lax.psum(negative_part, 'grp')]
    ppermute x0 -> x16, starting transfers between devices: none -> 18.4 us  [the longest x14 15.3 us: swap(): return lax.ppermute(x, axis, [(i, i ^ mask) for i in range(count)])]
    pmax x1 -> x0, blocking collectives: 17 us -> none  [log_total(): row_max = lax.pmax(maxima, 'dev')]
    all_gather x1 -> x0, blocking collectives: 16.7 us -> none  [local(): group_q = lax.all_gather(queries, 'dev', axis=0, tiled=True)]
    psum x1 -> x0, blocking collectives: 13.6 us -> none  [log_total(): row_sum = lax.psum(totals * jnp.exp(maxima - row_max), 'dev')]
    pallas_call x0 -> x6, Pallas kernels: none -> 7.24 us  [call(): pl.pallas_call(kernel, out_shape=shapes, in_specs=specs, out_specs=[spec]...]
    ppermute x0 -> x16, waiting for transfers between devices: none -> 6.46 us  [the longest x14 5.89 us: swap(): return lax.ppermute(x, axis, [(i, i ^ mask) for i in range(count)])]
    dot_general x8 -> x0, matrix products: 4.02 us -> none  [the longest x4 2.24 us: logits(): jnp.dot(q_block, candidates.T, preferred_element_type=jnp.float32)]
  transfers between devices with their start and end apart: 2 -> 16, of which waited for: 1 -> 6; matrix products, arithmetic and copies ran while one was open for 1% -> 3% of each run, Pallas kernels for 0% -> 13%
where the time goes in v2:
time: 39.8 us; the launch traced here: 39.5 us
  starting transfers between devices  18.4 us (46%)
  Pallas kernels  7.24 us (18%)
  waiting for transfers between devices  6.46 us (16%)
  local copies, waits for them, and re-layouts  5.04 us (13%)
  other arithmetic  1.65 us (4%)
  between operations  0.72 us (2%)
    ppermute x14, starting transfers between devices, swap(): return lax.ppermute(x, axis, [(i, i ^ mask) for i in range(count)])  15.3 us
    pallas_call x6, Pallas kernels, call(): pl.pallas_call(kernel, out_shape=shapes, in_specs=specs, out_specs=[spec]...  7.24 us
    ppermute x14, waiting for transfers between devices, swap(): return lax.ppermute(x, axis, [(i, i ^ mask) for i in range(count)])  5.89 us
    unnamed x13, local copies, waits for them, and re-layouts  5.04 us
    ppermute x2, starting transfers between devices, butterfly(): return lax.ppermute(x, ('grp', 'dev'), pairs)  3.14 us
    add x1, other arithmetic, step(): total = part.astype(F32) + other.astype(F32)  0.85 us
  transfers between devices with their start and end apart: 16, of which 6 were waited for; matrix products, arithmetic and copies ran while one was open for 3% of the time, Pallas kernels for 13%

profile of v2, /device:TPU:0, one launch (start us, length us, event | category | flops | bytes accessed | tf_op | source)
XLA Modules:
  0.0 39.5 jit_solution(9587950365329774953)
XLA Ops:
  0.6 0.6 %collective-permute-start.1 = (bf16[512,256]{1,0:T(8,128)(2,1)}, bf16[512,256]{1,0:T(8,128)(2,1)S(1)}, u32[]{:S(2)}, u32[]{:S(2)}) collective-permute-start(bf16[512,256]{1,0:T(8,128)(2,1)} %refs_1_.1), channel_id=1, source_target_pairs={{0,1},{1,0},{2,3},{3,2},{4,5},{5,4},{6,7},{7,6},{8,9},{9,8},{10,11... | collective-permute-start | bytes 786440 | tf_op jit(solution)/shard_map/ppermute | solution.py:20
  1.3 0.4 %collective-permute-start.2 = (f32[512]{0:T(512)}, f32[512]{0:T(512)S(1)}, u32[]{:S(2)}, u32[]{:S(2)}) collective-permute-start(f32[512]{0:T(512)} %param.10), channel_id=1, source_target_pairs={{0,1},{1,0},{2,3},{3,2},{4,5},{5,4},{6,7},{7,6},{8,9},{9,8},{10,11... | collective-permute-start | bytes 6152 | tf_op jit(solution)/shard_map/ppermute | solution.py:20
  1.7 2.6 %collective-permute-start.3 = (bf16[128,256]{1,0:T(8,128)(2,1)}, bf16[128,256]{1,0:T(8,128)(2,1)S(1)}, u32[]{:S(2)}, u32[]{:S(2)}) collective-permute-start(bf16[128,256]{1,0:T(8,128)(2,1)} %q_ref.1), channel_id=1, source_target_pairs={{0,2},{1,3},{2,0},{3,1},{4,6},{5,7},{6,4},{7,5},{8,10},{9,11},{10,... | collective-permute-start | bytes 196616 | tf_op jit(solution)/shard_map/ppermute | solution.py:20
  4.3 2.5 %collective-permute-start.5 = (bf16[128,256]{1,0:T(8,128)(2,1)}, bf16[128,256]{1,0:T(8,128)(2,1)S(1)}, u32[]{:S(2)}, u32[]{:S(2)}) collective-permute-start(bf16[128,256]{1,0:T(8,128)(2,1)} %q_ref.1), channel_id=1, source_target_pairs={{0,6},{1,7},{2,4},{3,5},{4,2},{5,3},{6,0},{7,1},{8,14},{9,15},{10,... | collective-permute-start | bytes 196616 | tf_op jit(solution)/shard_map/ppermute | solution.py:20
  7.0 1.2 %copy-done = f32[262144]{0:T(1024)S(1)} copy-done((f32[262144]{0:T(1024)S(1)}, f32[262144]{0:T(1024)}, u32[]{:S(2)}) %copy-start) | copy-done | bytes 1048600
  8.2 0.9 %copy-done.1 = bf16[512,256]{1,0:T(8,128)(2,1)S(1)} copy-done((bf16[512,256]{1,0:T(8,128)(2,1)S(1)}, bf16[512,256]{1,0:T(8,128)(2,1)}, u32[]{:S(2)}) %copy-start.1) | copy-done | bytes 262168
  9.1 0.8 %copy-done.2 = bf16[128,256]{1,0:T(8,128)(2,1)S(1)} copy-done((bf16[128,256]{1,0:T(8,128)(2,1)S(1)}, bf16[128,256]{1,0:T(8,128)(2,1)}, u32[]{:S(2)}) %copy-start.2) | copy-done | bytes 65560
  10.0 0.8 %copy-done.3 = bf16[128,256]{1,0:T(8,128)(2,1)S(1)} copy-done((bf16[128,256]{1,0:T(8,128)(2,1)S(1)}, bf16[128,256]{1,0:T(8,128)(2,1)}, u32[]{:S(2)}) %copy-start.3) | copy-done | bytes 65560
  10.8 0.7 %copy-done.5 = f32[512]{0:T(512)S(1)} copy-done((f32[512]{0:T(512)S(1)}, f32[512]{0:T(512)}, u32[]{:S(2)}) %copy-start.5) | copy-done | bytes 2072
  11.5 2.0 %shard_map.93 = (f32[1,128]{1,0:T(1,128)S(1)}, f32[128,128]{1,0:T(8,128)S(1)}, bf16[256,1280]{1,0:T(8,128)(2,1)S(1)}, bf16[128,256]{1,0:T(8,128)(2,1)S(1)}, bf16...) custom-call(s32[1024]{0:T(1024)S(1)} %copy-done.4, f32[2048,128]{1,0:T(8,128)S(1)} %bitcast.5, ...), custom_call_target="tpu_custom_call" | custom-call | flops 83886080 | tf_op jit(solution)/shard_map/pallas_call | solution.py:227
  13.5 0.3 collective-permute-done.4.r_1_.r_2_
  13.8 1.0 %shard_map.94 = (f32[4,128]{1,0:T(4,128)S(1)}, bf16[16,128]{1,0:T(8,128)(2,1)S(1)}) custom-call(bf16[128,256]{1,0:T(8,128)(2,1)S(1)} %collective-permute-done.3.r_0_.r_1_, bf16[128,256]{1,0:T(8,128)(2,1)S(1)} %collective-permute-done.4.r_1_.r_2_, bf16[128,256]{1,0:T(8,128)(2,1)S(1)} %collective-permute-done.5.r_2_.r_3_, ...), custom_call_target="tpu_custom_call" | custom-call | flops 251658240 | tf_op jit(solution)/shard_map/pallas_call | solution.py:227
  14.8 2.8 %collective-permute-start.8 = (bf16[16,128]{1,0:T(8,128)(2,1)S(1)}, bf16[16,128]{1,0:T(8,128)(2,1)S(1)}, u32[]{:S(2)}, u32[]{:S(2)}) collective-permute-start(bf16[16,128]{1,0:T(8,128)(2,1)S(1)} %get-tuple-element.31), channel_id=1, source_target_pairs={{0,6},{1,7},{2,4},{3,5},{4,2},{5,3},{6,0},{7,1},{8,14},{9,15},{10,... | collective-permute-start | bytes 12296 | tf_op jit(solution)/shard_map/ppermute | solution.py:20
  17.6 0.3 collective-permute-start.7
  17.9 1.4 %collective-permute-start.6 = (bf16[16,128]{1,0:T(8,128)(2,1)S(1)}, bf16[16,128]{1,0:T(8,128)(2,1)S(1)}, u32[]{:S(2)}, u32[]{:S(2)}) collective-permute-start(bf16[16,128]{1,0:T(8,128)(2,1)S(1)} %get-tuple-element.31), channel_id=1, source_target_pairs={{0,2},{1,3},{2,0},{3,1},{4,6},{5,7},{6,4},{7,5},{8,10},{9,11},{10,... | collective-permute-start | bytes 12296 | tf_op jit(solution)/shard_map/ppermute | solution.py:20
  19.2 1.0 %collective-permute-done.8.r_9_ = bf16[16,128]{1,0:T(8,128)(2,1)S(1)} collective-permute-done((bf16[16,128]{1,0:T(8,128)(2,1)S(1)}, bf16[16,128]{1,0:T(8,128)(2,1)S(1)}, u32[]{:S(2)}, u32[]{:S(2)}) %collective-permute-start.8) | collective-permute-done | bytes 4128 | tf_op jit(solution)/shard_map/ppermute | solution.py:20
  20.3 1.8 %collective-permute-done.7.r_8_ = bf16[16,128]{1,0:T(8,128)(2,1)S(1)} collective-permute-done((bf16[16,128]{1,0:T(8,128)(2,1)S(1)}, bf16[16,128]{1,0:T(8,128)(2,1)S(1)}, u32[]{:S(2)}, u32[]{:S(2)}) %collective-permute-start.7) | collective-permute-done | bytes 4128 | tf_op jit(solution)/shard_map/ppermute | solution.py:20
  22.1 1.1 %shard_map.95 = (bf16[512,256]{1,0:T(8,128)(2,1)S(1)}, bf16[512,512]{1,0:T(8,128)(2,1)S(1)}, f32[4,128]{1,0:T(4,128)S(1)}, bf16[512,256]{1,0:T(8,128)(2,1)S(1)}) custom-call(bf16[128,256]{1,0:T(8,128)(2,1)S(1)} %get-tuple-element.25.r_0_, bf16[128,256]{1,0:T(8,128)(2,1)S(1)} %collective-permute-done.3.r_0_.r_1_, ...), custom_call_target="tpu_custom_call" | custom-call | flops 268435456 | tf_op jit(solution)/shard_map/pallas_call | solution.py:227
  23.2 1.1 %shard_map.96 = (f32[512,256]{1,0:T(8,128)S(1)}, bf16[512,512]{1,0:T(8,128)(2,1)S(1)}) custom-call(bf16[512,256]{1,0:T(8,128)(2,1)S(1)} %get-tuple-element.32.r_0_, bf16[512,256]{1,0:T(8,128)(2,1)S(1)} %get-tuple-element.28.r_5_.r_1_, f32[128,128]{1,0:T(8,128)S(1)} %get-tuple-element.26.r_7_.r_5_.r_2_.r_3_, f32[4,128]{1,0:T(4,128)S(1)} %get-tuple-element.33.r_3_.r_4_), custom_call_target="tpu_custom_call" | custom-call | flops 268435456 | tf_op jit(solution)/shard_map/pallas_call | solution.py:227
  24.3 0.5 %collective-permute-done.9 = bf16[512,256]{1,0:T(8,128)(2,1)S(1)} collective-permute-done((bf16[512,256]{1,0:T(8,128)(2,1)S(1)}, bf16[512,256]{1,0:T(8,128)(2,1)S(1)}, u32[]{:S(2)}, u32[]{:S(2)}) %collective-permute-start.9) | collective-permute-done | bytes 262176 | tf_op jit(solution)/shard_map/ppermute | solution.py:20
  24.8 1.6 %collective-permute-start.14 = (bf16[512,256]{1,0:T(8,128)(2,1)S(1)}, bf16[512,256]{1,0:T(8,128)(2,1)S(1)}, u32[]{:S(2)}, u32[]{:S(2)}) collective-permute-start(bf16[512,256]{1,0:T(8,128)(2,1)S(1)} %add_convert_fusion.1.r_8_), channel_id=1, source_target_pairs={{0,8},{1,17},{2,10},{3,19},{4,12},{5,21},{6,14},{7,23},{8,0},{9,25... | collective-permute-start | bytes 786440 | tf_op jit(solution)/shard_map/ppermute | solution.py:244
  26.4 1.3 %shard_map.97 = (f32[1,128]{1,0:T(1,128)S(1)}, f32[128,256]{1,0:T(8,128)S(1)}, bf16[128,256]{1,0:T(8,128)(2,1)S(1)}, f32[256,128]{1,0:T(8,128)S(1)}, bf16[256,12...) custom-call(bf16[512,256]{1,0:T(8,128)(2,1)S(1)} %get-tuple-element.32.r_0_, ...), custom_call_target="tpu_custom_call" | custom-call | flops 1006632960 | tf_op jit(solution)/shard_map/pallas_call | solution.py:227
  27.7 0.9 %collective-permute-start.10 = (bf16[256,128]{1,0:T(8,128)(2,1)S(1)}, bf16[256,128]{1,0:T(8,128)(2,1)S(1)}, u32[]{:S(2)}, u32[]{:S(2)}) collective-permute-start(bf16[256,128]{1,0:T(8,128)(2,1)S(1)} %get-tuple-element.41), channel_id=1, source_target_pairs={{0,2},{1,3},{2,0},{3,1},{4,6},{5,7},{6,4},{7,5},{8,10},{9,11},{10,... | collective-permute-start | bytes 196616 | tf_op jit(solution)/shard_map/ppermute | solution.py:20
  28.6 1.6 %collective-permute-start.11 = (bf16[256,128]{1,0:T(8,128)(2,1)S(1)}, bf16[256,128]{1,0:T(8,128)(2,1)S(1)}, u32[]{:S(2)}, u32[]{:S(2)}) collective-permute-start(bf16[256,128]{1,0:T(8,128)(2,1)S(1)} %get-tuple-element.42), channel_id=1, source_target_pairs={{0,4},{1,5},{2,6},{3,7},{4,0},{5,1},{6,2},{7,3},{8,12},{9,13},{10,... | collective-permute-start | bytes 196616 | tf_op jit(solution)/shard_map/ppermute | solution.py:20
  30.2 2.0 %collective-permute-start.12 = (bf16[256,128]{1,0:T(8,128)(2,1)S(1)}, bf16[256,128]{1,0:T(8,128)(2,1)S(1)}, u32[]{:S(2)}, u32[]{:S(2)}) collective-permute-start(bf16[256,128]{1,0:T(8,128)(2,1)S(1)} %get-tuple-element.43), channel_id=1, source_target_pairs={{0,6},{1,7},{2,4},{3,5},{4,2},{5,3},{6,0},{7,1},{8,14},{9,15},{10,... | collective-permute-start | bytes 196616 | tf_op jit(solution)/shard_map/ppermute | solution.py:20
  32.2 1.6 %collective-permute-start.15 = (bf16[512,256]{1,0:T(8,128)(2,1)S(1)}, bf16[512,256]{1,0:T(8,128)(2,1)S(1)}, u32[]{:S(2)}, u32[]{:S(2)}) collective-permute-start(bf16[512,256]{1,0:T(8,128)(2,1)S(1)} %add_convert_fusion), channel_id=1, source_target_pairs={{0,16},{1,9},{2,18},{3,11},{4,20},{5,13},{6,22},{7,15},{8,24},{9,1... | collective-permute-start | bytes 786440 | tf_op jit(solution)/shard_map/ppermute | solution.py:244
  33.8 0.5 %copy.10 = f32[128]{0:T(128)} copy(f32[128]{0:T(128)S(1)} %bitcast.4) | data formatting | bytes 1024
  34.3 2.3 %collective-permute-done.11.refs_1_ = bf16[256,128]{1,0:T(8,128)(2,1)S(1)} collective-permute-done((bf16[256,128]{1,0:T(8,128)(2,1)S(1)}, bf16[256,128]{1,0:T(8,128)(2,1)S(1)}, u32[]{:S(2)}, u32[]{:S(2)}) %collective-permute-start.11) | collective-permute-done | bytes 65568 | tf_op jit(solution)/shard_map/ppermute | solution.py:20
  36.7 0.8 %shard_map.98 = f32[128,256]{1,0:T(8,128)} custom-call(f32[256,128]{1,0:T(8,128)S(1)} %get-tuple-element.40.own_ref, bf16[256,128]{1,0:T(8,128)(2,1)S(1)} %collective-permute-done.10.refs_0_, bf16[256,128]{1,0:T(8,128)(2,1)S(1)} %collective-permute-done.11.refs_1_, bf16[256,128]{1,0:T(8,128)(2,1)S(1)} %collective-permute-done.12.refs_2_), custom_call_target="tpu_custom_call" | custom-call | flops 131072 | tf_op jit(solution)/shard_map/pallas_call | solution.py:227
  37.4 0.7 %convert_add_fusion.1 = f32[128,256]{1,0:T(8,128)} fusion(f32[128,256]{1,0:T(8,128)S(1)} %get-tuple-element.44, bf16[128,256]{1,0:T(8,128)(2,1)S(1)} %collective-permute-done.13), kind=kLoop, calls=%fused_computation.3 | loop fusion | flops 65536 | bytes 327680 | tf_op jit(solution)/shard_map/add | solution.py:327
  38.1 0.6 %collective-permute-done.15 = bf16[512,256]{1,0:T(8,128)(2,1)S(1)} collective-permute-done((bf16[512,256]{1,0:T(8,128)(2,1)S(1)}, bf16[512,256]{1,0:T(8,128)(2,1)S(1)}, u32[]{:S(2)}, u32[]{:S(2)}) %collective-permute-start.15) | collective-permute-done | bytes 262176 | tf_op jit(solution)/shard_map/ppermute | solution.py:244
  38.7 0.8 %convert_add_fusion = f32[512,256]{1,0:T(8,128)} fusion(bf16[512,256]{1,0:T(8,128)(2,1)S(1)} %collective-permute-done.15, bf16[512,256]{1,0:T(8,128)(2,1)S(1)} %add_convert_fusion), kind=kLoop, calls=%fused_computation | loop fusion | flops 393216 | bytes 1048576 | tf_op jit(solution)/shard_map/add | solution.py:325
  (23 shorter events, 0.4 us)
Async XLA Ops:
  0.6 6.3 %copy-start.4 = (s32[1024]{0:T(1024)S(1)}, s32[1024]{0:T(1024)}, u32[]{:S(2)}) copy-start(s32[1024]{0:T(1024)} %ids_ref.1) | copy-start | bytes 12292
  0.6 6.3 %collective-permute-start.1 = (bf16[512,256]{1,0:T(8,128)(2,1)}, bf16[512,256]{1,0:T(8,128)(2,1)S(1)}, u32[]{:S(2)}, u32[]{:S(2)}) collective-permute-start(bf16[512,256]{1,0:T(8,128)(2,1)} %refs_1_.1), channel_id=1, source_target_pairs={{0,1},{1,0},{2,3},{3,2},{4,5},{5,4},{6,7},{7,6},{8,9},{9,8},{10,11... | collective-permute-start | bytes 786440 | tf_op jit(solution)/shard_map/ppermute | solution.py:20
  1.2 5.7 %collective-permute-start = (bf16[128,256]{1,0:T(8,128)(2,1)}, bf16[128,256]{1,0:T(8,128)(2,1)S(1)}, u32[]{:S(2)}, u32[]{:S(2)}) collective-permute-start(bf16[128,256]{1,0:T(8,128)(2,1)} %refs_0_.1), channel_id=1, source_target_pairs={{0,1},{1,0},{2,3},{3,2},{4,5},{5,4},{6,7},{7,6},{8,9},{9,8},{10,11... | collective-permute-start | bytes 196616 | tf_op jit(solution)/shard_map/ppermute | solution.py:20
  1.3 5.5 %collective-permute-start.2 = (f32[512]{0:T(512)}, f32[512]{0:T(512)S(1)}, u32[]{:S(2)}, u32[]{:S(2)}) collective-permute-start(f32[512]{0:T(512)} %param.10), channel_id=1, source_target_pairs={{0,1},{1,0},{2,3},{3,2},{4,5},{5,4},{6,7},{7,6},{8,9},{9,8},{10,11... | collective-permute-start | bytes 6152 | tf_op jit(solution)/shard_map/ppermute | solution.py:20
  1.7 11.8 %collective-permute-start.3 = (bf16[128,256]{1,0:T(8,128)(2,1)}, bf16[128,256]{1,0:T(8,128)(2,1)S(1)}, u32[]{:S(2)}, u32[]{:S(2)}) collective-permute-start(bf16[128,256]{1,0:T(8,128)(2,1)} %q_ref.1), channel_id=1, source_target_pairs={{0,2},{1,3},{2,0},{3,1},{4,6},{5,7},{6,4},{7,5},{8,10},{9,11},{10,... | collective-permute-start | bytes 196616 | tf_op jit(solution)/shard_map/ppermute | solution.py:20
  4.3 9.2 %collective-permute-start.5 = (bf16[128,256]{1,0:T(8,128)(2,1)}, bf16[128,256]{1,0:T(8,128)(2,1)S(1)}, u32[]{:S(2)}, u32[]{:S(2)}) collective-permute-start(bf16[128,256]{1,0:T(8,128)(2,1)} %q_ref.1), channel_id=1, source_target_pairs={{0,6},{1,7},{2,4},{3,5},{4,2},{5,3},{6,0},{7,1},{8,14},{9,15},{10,... | collective-permute-start | bytes 196616 | tf_op jit(solution)/shard_map/ppermute | solution.py:20
  6.8 7.0 %collective-permute-start.4 = (bf16[128,256]{1,0:T(8,128)(2,1)}, bf16[128,256]{1,0:T(8,128)(2,1)S(1)}, u32[]{:S(2)}, u32[]{:S(2)}) collective-permute-start(bf16[128,256]{1,0:T(8,128)(2,1)} %q_ref.1), channel_id=1, source_target_pairs={{0,4},{1,5},{2,6},{3,7},{4,0},{5,1},{6,2},{7,3},{8,12},{9,13},{10,... | collective-permute-start | bytes 196616 | tf_op jit(solution)/shard_map/ppermute | solution.py:20
  7.0 1.2 %copy-start = (f32[262144]{0:T(1024)S(1)}, f32[262144]{0:T(1024)}, u32[]{:S(2)}) copy-start(f32[262144]{0:T(1024)} %param.11) | copy-start | bytes 3145732
  8.2 0.9 %copy-start.1 = (bf16[512,256]{1,0:T(8,128)(2,1)S(1)}, bf16[512,256]{1,0:T(8,128)(2,1)}, u32[]{:S(2)}) copy-start(bf16[512,256]{1,0:T(8,128)(2,1)} %refs_1_.1) | copy-start | bytes 786436
  9.1 0.8 %copy-start.2 = (bf16[128,256]{1,0:T(8,128)(2,1)S(1)}, bf16[128,256]{1,0:T(8,128)(2,1)}, u32[]{:S(2)}) copy-start(bf16[128,256]{1,0:T(8,128)(2,1)} %refs_0_.1) | copy-start | bytes 196612
  10.0 0.8 %copy-start.3 = (bf16[128,256]{1,0:T(8,128)(2,1)S(1)}, bf16[128,256]{1,0:T(8,128)(2,1)}, u32[]{:S(2)}) copy-start(bf16[128,256]{1,0:T(8,128)(2,1)} %q_ref.1) | copy-start | bytes 196612
  10.8 0.7 %copy-start.5 = (f32[512]{0:T(512)S(1)}, f32[512]{0:T(512)}, u32[]{:S(2)}) copy-start(f32[512]{0:T(512)} %param.10) | copy-start | bytes 6148
  14.8 5.5 %collective-permute-start.8 = (bf16[16,128]{1,0:T(8,128)(2,1)S(1)}, bf16[16,128]{1,0:T(8,128)(2,1)S(1)}, u32[]{:S(2)}, u32[]{:S(2)}) collective-permute-start(bf16[16,128]{1,0:T(8,128)(2,1)S(1)} %get-tuple-element.31), channel_id=1, source_target_pairs={{0,6},{1,7},{2,4},{3,5},{4,2},{5,3},{6,0},{7,1},{8,14},{9,15},{10,... | collective-permute-start | bytes 12296 | tf_op jit(solution)/shard_map/ppermute | solution.py:20
  17.6 4.5 %collective-permute-start.7 = (bf16[16,128]{1,0:T(8,128)(2,1)S(1)}, bf16[16,128]{1,0:T(8,128)(2,1)S(1)}, u32[]{:S(2)}, u32[]{:S(2)}) collective-permute-start(bf16[16,128]{1,0:T(8,128)(2,1)S(1)} %get-tuple-element.31), channel_id=1, source_target_pairs={{0,4},{1,5},{2,6},{3,7},{4,0},{5,1},{6,2},{7,3},{8,12},{9,13},{10,... | collective-permute-start | bytes 12296 | tf_op jit(solution)/shard_map/ppermute | solution.py:20
  17.9 4.2 %collective-permute-start.6 = (bf16[16,128]{1,0:T(8,128)(2,1)S(1)}, bf16[16,128]{1,0:T(8,128)(2,1)S(1)}, u32[]{:S(2)}, u32[]{:S(2)}) collective-permute-start(bf16[16,128]{1,0:T(8,128)(2,1)S(1)} %get-tuple-element.31), channel_id=1, source_target_pairs={{0,2},{1,3},{2,0},{3,1},{4,6},{5,7},{6,4},{7,5},{8,10},{9,11},{10,... | collective-permute-start | bytes 12296 | tf_op jit(solution)/shard_map/ppermute | solution.py:20
  23.1 1.6 %collective-permute-start.9 = (bf16[512,256]{1,0:T(8,128)(2,1)S(1)}, bf16[512,256]{1,0:T(8,128)(2,1)S(1)}, u32[]{:S(2)}, u32[]{:S(2)}) collective-permute-start(bf16[512,256]{1,0:T(8,128)(2,1)S(1)} %get-tuple-element.38), channel_id=1, source_target_pairs={{0,1},{1,0},{2,3},{3,2},{4,5},{5,4},{6,7},{7,6},{8,9},{9,8},{10,11... | collective-permute-start | bytes 786440 | tf_op jit(solution)/shard_map/ppermute | solution.py:20
  24.8 7.3 %collective-permute-start.14 = (bf16[512,256]{1,0:T(8,128)(2,1)S(1)}, bf16[512,256]{1,0:T(8,128)(2,1)S(1)}, u32[]{:S(2)}, u32[]{:S(2)}) collective-permute-start(bf16[512,256]{1,0:T(8,128)(2,1)S(1)} %add_convert_fusion.1.r_8_), channel_id=1, source_target_pairs={{0,8},{1,17},{2,10},{3,19},{4,12},{5,21},{6,14},{7,23},{8,0},{9,25... | collective-permute-start | bytes 786440 | tf_op jit(solution)/shard_map/ppermute | solution.py:244
  27.7 6.6 %collective-permute-start.10 = (bf16[256,128]{1,0:T(8,128)(2,1)S(1)}, bf16[256,128]{1,0:T(8,128)(2,1)S(1)}, u32[]{:S(2)}, u32[]{:S(2)}) collective-permute-start(bf16[256,128]{1,0:T(8,128)(2,1)S(1)} %get-tuple-element.41), channel_id=1, source_target_pairs={{0,2},{1,3},{2,0},{3,1},{4,6},{5,7},{6,4},{7,5},{8,10},{9,11},{10,... | collective-permute-start | bytes 196616 | tf_op jit(solution)/shard_map/ppermute | solution.py:20
  28.6 8.1 %collective-permute-start.11 = (bf16[256,128]{1,0:T(8,128)(2,1)S(1)}, bf16[256,128]{1,0:T(8,128)(2,1)S(1)}, u32[]{:S(2)}, u32[]{:S(2)}) collective-permute-start(bf16[256,128]{1,0:T(8,128)(2,1)S(1)} %get-tuple-element.42), channel_id=1, source_target_pairs={{0,4},{1,5},{2,6},{3,7},{4,0},{5,1},{6,2},{7,3},{8,12},{9,13},{10,... | collective-permute-start | bytes 196616 | tf_op jit(solution)/shard_map/ppermute | solution.py:20
  30.2 6.5 %collective-permute-start.12 = (bf16[256,128]{1,0:T(8,128)(2,1)S(1)}, bf16[256,128]{1,0:T(8,128)(2,1)S(1)}, u32[]{:S(2)}, u32[]{:S(2)}) collective-permute-start(bf16[256,128]{1,0:T(8,128)(2,1)S(1)} %get-tuple-element.43), channel_id=1, source_target_pairs={{0,6},{1,7},{2,4},{3,5},{4,2},{5,3},{6,0},{7,1},{8,14},{9,15},{10,... | collective-permute-start | bytes 196616 | tf_op jit(solution)/shard_map/ppermute | solution.py:20
  32.1 5.3 %collective-permute-start.13 = (bf16[128,256]{1,0:T(8,128)(2,1)S(1)}, bf16[128,256]{1,0:T(8,128)(2,1)S(1)}, u32[]{:S(2)}, u32[]{:S(2)}) collective-permute-start(bf16[128,256]{1,0:T(8,128)(2,1)S(1)} %get-tuple-element.45), channel_id=1, source_target_pairs={{0,1},{1,0},{2,3},{3,2},{4,5},{5,4},{6,7},{7,6},{8,9},{9,8},{10,11... | collective-permute-start | bytes 196616 | tf_op jit(solution)/shard_map/ppermute | solution.py:20
  32.2 6.4 %collective-permute-start.15 = (bf16[512,256]{1,0:T(8,128)(2,1)S(1)}, bf16[512,256]{1,0:T(8,128)(2,1)S(1)}, u32[]{:S(2)}, u32[]{:S(2)}) collective-permute-start(bf16[512,256]{1,0:T(8,128)(2,1)S(1)} %add_convert_fusion), channel_id=1, source_target_pairs={{0,16},{1,9},{2,18},{3,11},{4,20},{5,13},{6,22},{7,15},{8,24},{9,1... | collective-permute-start | bytes 786440 | tf_op jit(solution)/shard_map/ppermute | solution.py:244

commit v3 on v2

v3 whole, which is shorter than its diff:
```python
import jax
import jax.numpy as jnp
from jax import lax
from jax.experimental import pallas as pl
from jax.experimental.pallas import tpu as pltpu
from jax.sharding import PartitionSpec as P

logit_scale = 0.25
LANES = 128
F32, BF16 = jnp.float32, jnp.bfloat16
NT = (((1,), (1,)), ((), ()))
GRANT = 16 << 20


def round_up(x, m):
    return -(-x // m) * m


def swap(x, axis, count, mask):
    return lax.ppermute(x, axis, [(i, i ^ mask) for i in range(count)])


def fold(x, op):
    rows, cols = x.shape
    return op(x.reshape(rows // 8, 8, cols), axis=0)


def pad_rows(parts, multiple):
    have = sum(p.shape[0] for p in parts)
    lack = round_up(have, multiple) - have
    if lack:
        parts = parts + [jnp.zeros((lack, parts[0].shape[1]), parts[0].dtype)]
    return jnp.concatenate(parts, axis=0)


def split3(x):
    hi = x.astype(BF16)
    rest = x - hi.astype(F32)
    mid = rest.astype(BF16)
    return [hi, mid, (rest - mid.astype(F32)).astype(BF16)]


def runs_of(refs, rows):
    return [(ref, first) for ref in refs for first in range(0, ref.shape[0], rows)]


def prepare_kernel(ids_ref, table_hbm, q_hbm, it_hbm, neg_hbm, lq_hbm, *refs):
    q_ref, it_ref, neg_ref, cols_ref, table, lq, picked, sems = refs
    copies = [
        pltpu.make_async_copy(src, dst, sems.at[i])
        for i, (src, dst) in enumerate(
            [(table_hbm, table), (lq_hbm, lq), (q_hbm, q_ref), (it_hbm, it_ref), (neg_hbm, neg_ref)]
        )
    ]
    for c in copies:
        c.start()
    copies[0].wait()
    copies[1].wait()
    rows, _ = q_ref.shape
    dev = lax.axis_index("dev")
    lane = lax.broadcasted_iota(jnp.int32, (1, LANES), 1)
    for half, owner in enumerate((dev, dev ^ 1)):
        start = owner * rows

        def pick(i, carry, half=half, start=start):
            for t in range(8):
                j = i * 8 + t
                item = ids_ref[start + j]
                row = table[pl.ds(lax.shift_right_logical(item, 7), 1), :]
                picked[pl.ds(half * rows + j, 1), :] = jnp.where(lane == (item & (LANES - 1)), row, 0.0)
            return carry

        lax.fori_loop(0, rows // 8, pick, 0)
    for half in range(2):
        part = picked[half * rows : (half + 1) * rows, :]
        cols_ref[:, half : half + 1] = jnp.sum(part, axis=1, keepdims=True)
    own = lq.shape[0]
    cols_ref[:, 2 : 2 + own] = pad_rows([lq[...]], 8).T[:, :own]
    for c in copies[2:]:
        c.wait()


def first_pass(runs, cols, q, e_ref, diagonal):
    rows = q.shape[0]
    top, matched = None, None
    for j, (ref, first) in enumerate(runs):
        s = lax.dot_general(ref[first : first + rows, :], q, NT, preferred_element_type=F32)
        s = logit_scale * s - cols[j]
        e_ref[j * rows : (j + 1) * rows, :] = s
        here = fold(s, jnp.max)
        top = here if top is None else jnp.maximum(top, here)
        if diagonal and j == 0:
            matched = jnp.sum(jnp.where(own_mask(rows), s, 0.0), axis=0, keepdims=True)
    row_max = jnp.max(top, axis=0, keepdims=True)
    total = None
    for j in range(len(runs)):
        e = jnp.exp(e_ref[j * rows : (j + 1) * rows, :] - row_max)
        e_ref[j * rows : (j + 1) * rows, :] = e
        here = fold(e, jnp.sum)
        total = here if total is None else total + here
    return row_max, row_max + jnp.log(jnp.sum(total, axis=0, keepdims=True)), matched


def own_mask(rows):
    shape = (rows, rows)
    return lax.broadcasted_iota(jnp.int32, shape, 0) == lax.broadcasted_iota(jnp.int32, shape, 1)


def candidate_cols(own_ref, partner_ref, negs):
    return (
        [own_ref[:, j : j + 1] for j in range(2 + negs)]
        + [partner_ref[:, j : j + 1] for j in range(negs)]
    )


def own_block_kernel(q_ref, it_o, it_p, neg_o, neg_p, cols_own, lq_p, *refs):
    stat_ref, e_ref, ct_ref, cols_ref = refs
    rows, _ = q_ref.shape
    negs = lq_p.shape[0]
    cols_ref[:, :negs] = pad_rows([lq_p[...]], 8).T[:, :negs]
    runs = runs_of((it_o, it_p, neg_o, neg_p), rows)
    cols = candidate_cols(cols_own, cols_ref, negs)
    stat_ref[0:1, :], stat_ref[1:2, :], stat_ref[2:3, :] = first_pass(runs, cols, q_ref[...], e_ref, True)
    for j, (ref, first) in enumerate(runs):
        ct_ref[:, j * rows : (j + 1) * rows] = ref[first : first + rows, :].T


def other_blocks_kernel(n, *refs):
    q_refs, refs = refs[: n - 1], refs[n - 1 :]
    c_refs, (cols_own, cols_par, stat0_ref), refs = refs[:4], refs[4:7], refs[7:]
    max_ref, lse_ref, msg_ref, e_refs = refs[0], refs[1], refs[2], refs[3:]
    rows, _ = q_refs[0].shape
    runs = runs_of(c_refs, rows)
    cols = candidate_cols(cols_own, cols_par, c_refs[2].shape[0] // rows)
    max_ref[0:1, :] = stat0_ref[0:1, :]
    lse_ref[0:1, :] = stat0_ref[1:2, :]
    for k in range(1, n):
        top, lse, _ = first_pass(runs, cols, q_refs[k - 1][...], e_refs[k - 1], False)
        max_ref[k : k + 1, :] = top
        lse_ref[k : k + 1, :] = lse
    msg_ref[...] = pad_rows(split3(lse_ref[...]), 16)


def second_pass(n, e_refs, offset, q_all, weight_ref, mask_first, p_ref, emit):
    rows = q_all.shape[0] // n
    for j in range(p_ref.shape[0] // rows):
        run = slice(j * rows, (j + 1) * rows)
        src = slice(offset + j * rows, offset + (j + 1) * rows)
        for b in range(n):
            p = e_refs[b][src, :] * weight_ref[b : b + 1, :]
            if mask_first and j == 0 and b == 0:
                p = p - jnp.where(own_mask(rows), logit_scale, 0.0)
            p_ref[run, b * rows : (b + 1) * rows] = p.astype(BF16)
        emit(j, jnp.dot(p_ref[run, :], q_all[...], preferred_element_type=F32))


def partner_kernel(n, offset, *refs):
    q_refs, e_refs, refs = refs[:n], refs[n : 2 * n], refs[2 * n :]
    max_ref, lse_ref, stat0_ref, refs = refs[0], refs[1], refs[2], refs[3:]
    got_refs, (out_ref, p_ref, weight_ref, loss_ref, q_all) = refs[: n - 1], refs[n - 1 :]
    rows, _ = q_refs[0].shape
    for k in range(n):
        q_all[k * rows : (k + 1) * rows, :] = q_refs[k][...]
    totals = [lse_ref[...]]
    for ref in got_refs:
        got = ref[...].astype(F32)
        totals.append(got[:n] + got[n : 2 * n] + got[2 * n : 3 * n])
    for b in range(n):
        parts = [totals[k][k ^ b : (k ^ b) + 1, :] for k in range(n)]
        top = parts[0]
        for r in parts[1:]:
            top = jnp.maximum(top, r)
        total = jnp.exp(parts[0] - top)
        for r in parts[1:]:
            total = total + jnp.exp(r - top)
        norm = top + jnp.log(total)
        weight_ref[b : b + 1, :] = logit_scale * jnp.exp(max_ref[b : b + 1, :] - norm)
        if b == 0:
            loss_ref[...] = norm - stat0_ref[2:3, :]

    def emit(j, g):
        out_ref[j * rows : (j + 1) * rows, :] = g.astype(BF16)

    second_pass(n, e_refs, offset, q_all, weight_ref, False, p_ref, emit)


def own_kernel(n, offset, q_all, weight_ref, *refs):
    e_refs, (out_ref, p_ref) = refs[:n], refs[n:]
    rows = q_all.shape[0] // n

    def emit(j, g):
        out_ref[j * rows : (j + 1) * rows, :] = g

    second_pass(n, e_refs, offset, q_all, weight_ref, False, p_ref, emit)


def items_kernel(n, q_all, weight_ref, ct_ref, p_own, p_par, _, *refs):
    e_refs, refs = refs[:n], refs[n:]
    (mine_ref, theirs_ref, own_ref), refs = refs[:3], refs[3:]
    msg_refs, (p_ref,) = refs[: n - 1], refs[n - 1 :]
    rows = q_all.shape[0] // n
    negs = p_own.shape[0]

    def emit(j, g):
        if j == 0:
            mine_ref[...] = g
        else:
            theirs_ref[...] = g.astype(BF16)

    second_pass(n, e_refs, 0, q_all, weight_ref, True, p_ref, emit)
    for k in range(n):
        part = slice(k * rows, (k + 1) * rows)
        u = jnp.dot(ct_ref[:, : 2 * rows], p_ref[:, part], preferred_element_type=F32)
        u += jnp.dot(ct_ref[:, 2 * rows : 2 * rows + negs], p_own[:, part], preferred_element_type=F32)
        u += jnp.dot(ct_ref[:, 2 * rows + negs :], p_par[:, part], preferred_element_type=F32)
        if k == 0:
            own_ref[...] = u
        else:
            msg_refs[k - 1][...] = u.astype(BF16)


def outputs_kernel(loss_in, mine_ref, back_ref, own_ref, *refs):
    loss_ref, query_ref, item_ref = refs[-3:]
    loss_ref[...] = loss_in[...]
    item_ref[...] = mine_ref[...] + back_ref[...].astype(F32)
    total = own_ref[...]
    for ref in refs[:-3]:
        total = total + ref[...].astype(F32)
    query_ref[...] = total.T


def local_fn(mesh):
    n_dev, n_grp = mesh.shape["dev"], mesh.shape["grp"]
    n = n_dev // 2
    masks = [1 << i for i in range((n_grp - 1).bit_length())]

    def call(kernel, outs, args, scratch, cost, specs=None):
        shapes = [o if isinstance(o, jax.ShapeDtypeStruct) else pltpu.VMEM(*o) for o in outs]
        vmem = pl.BlockSpec(memory_space=pltpu.VMEM)
        place = pltpu.VMEM if specs is None else pltpu.HBM
        flops, exps = cost
        return pl.pallas_call(
            kernel,
            out_shape=shapes,
            in_specs=specs or [vmem] * len(args),
            out_specs=[vmem] * len(outs),
            scratch_shapes=list(scratch),
            cost_estimate=pl.CostEstimate(flops=flops, bytes_accessed=0, transcendentals=exps),
            compiler_params=pltpu.CompilerParams(vmem_limit_bytes=GRANT),
        )(*[pltpu.with_memory_space_constraint(a, place) for a in args])

    def butterfly(x, t):
        steps = len(masks)
        pairs = []
        for g in range(n_grp):
            for d in range(n_dev):
                mask = masks[(t + d % 2) % steps]
                pairs.append((g * n_dev + d, (g ^ mask) * n_dev + d))
        return lax.ppermute(x, ("grp", "dev"), pairs)

    def local(queries, items, item_ids, neg_embed, neg_logq, logq_table):
        return step(queries, items, item_ids, neg_embed, neg_logq, logq_table)

    def exchange(x, k):
        return swap(x, "dev", n_dev, 2 * k)

    def partner(x):
        return swap(x, "dev", n_dev, 1)

    def step(queries, items, item_ids, neg_embed, neg_logq, logq_table):
        rows, width = queries.shape
        negs = neg_embed.shape[0]
        others = [exchange(queries, k) for k in range(1, n)]
        items_p = partner(items)
        neg_p = partner(neg_embed)
        logq_p = partner(neg_logq)
        cands = 2 * (rows + negs)
        unit = 2 * rows * width
        per_run = negs // rows
        shape = jax.ShapeDtypeStruct
        hbm = pl.BlockSpec(memory_space=pl.ANY)
        table_shape = (logq_table.size // LANES, LANES)

        q0, items, neg_embed, cols = call(
            prepare_kernel,
            [((rows, width), BF16), ((rows, width), BF16), ((negs, width), BF16), ((rows, LANES), F32)],
            (
                item_ids,
                logq_table.reshape(table_shape),
                queries,
                items,
                neg_embed,
                neg_logq.reshape(per_run, rows),
            ),
            [
                pltpu.VMEM(table_shape, F32),
                pltpu.VMEM((per_run, rows), F32),
                pltpu.VMEM((2 * rows, LANES), F32),
                pltpu.SemaphoreType.DMA((5,)),
            ],
            (rows * LANES, 0),
            [pl.BlockSpec(memory_space=pltpu.SMEM)] + [hbm] * 5,
        )
        cand_refs = (items, items_p, neg_embed, neg_p)
        stat0, e0, c_t, cols_p = call(
            own_block_kernel,
            [((3, rows), F32), ((cands, rows), F32), ((width, cands), BF16), ((rows, LANES), F32)],
            (q0, *cand_refs, cols, logq_p.reshape(per_run, rows)),
            (),
            (unit * cands, rows * cands),
        )
        msg_rows = round_up(3 * n, 16)
        tops, lse, msg, *e_rest = call(
            lambda *r: other_blocks_kernel(n, *r),
            [((n, rows), F32), ((n, rows), F32), ((msg_rows, rows), BF16)]
            + [((cands, rows), F32)] * (n - 1),
            (*others, *cand_refs, cols, cols_p, stat0),
            (),
            ((n - 1) * unit * cands, (n - 1) * rows * cands),
        )
        e = (e0, *e_rest)
        got = [exchange(msg, k) for k in range(1, n)]
        theirs, p_par, weight, loss, q_all = call(
            lambda *r: partner_kernel(n, 2 * rows + negs, *r),
            [
                ((negs, width), BF16),
                ((negs, n * rows), BF16),
                ((n, rows), F32),
                ((1, rows), F32),
                ((n * rows, width), BF16),
            ],
            (q0, *others, *e, tops, lse, stat0, *got),
            (),
            (n * unit * negs, 0),
        )
        back = partner(theirs)
        mine, p_own = call(
            lambda *r: own_kernel(n, 2 * rows, *r),
            [((negs, width), F32), ((negs, n * rows), BF16)],
            (q_all, weight, *e),
            (),
            (n * unit * negs, 0),
        )
        part = (mine + back.astype(F32)).astype(BF16)
        item_mine, item_theirs, u_own, *u_msgs = call(
            lambda *r: items_kernel(n, *r),
            [((rows, width), F32), ((rows, width), BF16), ((width, rows), F32)]
            + [((width, rows), BF16)] * (n - 1),
            (q_all, weight, c_t, p_own, p_par, part, *e),
            [pltpu.VMEM((2 * rows, n * rows), BF16)],
            (2 * n * unit * cands, 0),
        )
        item_back = partner(item_theirs)
        u_got = [exchange(u_msgs[k - 1], k) for k in range(1, n)]
        loss, query_grad, item_grad = call(
            outputs_kernel,
            [shape((1, rows), F32), shape((rows, width), F32), shape((rows, width), F32)],
            (loss, item_mine, item_back, u_own, *u_got),
            (),
            (n * rows * width, 0),
        )
        for t in range(len(masks)):
            other = butterfly(part, t)
            total = part.astype(F32) + other.astype(F32)
            part = total.astype(BF16)
        return (loss.reshape(rows), query_grad, item_grad, total)

    return local


def solution(mesh):
    return jax.shard_map(
        local_fn(mesh),
        mesh=mesh,
        in_specs=(
            P(("grp", "dev"), None),
            P(("grp", "dev"), None),
            P("grp"),
            P("dev", None),
            P("dev"),
            P(),
        ),
        out_specs=(
            P(("grp", "dev")),
            P(("grp", "dev"), None),
            P(("grp", "dev"), None),
            P("dev", None),
        ),
        check_vma=False,
    )
```

time: 39.8 us -> 44.2 us (1.11)
  waiting for transfers between devices: 6.46 us -> 17.1 us
  local copies, waits for them, and re-layouts: 5.04 us -> 0 us
  other arithmetic: 1.65 us -> 0.98 us
  Pallas kernels: 7.24 us -> 6.75 us
    ppermute x14, waiting for transfers between devices: 5.89 us -> 12.2 us  [swap(): return lax.ppermute(x, axis, [(i, i ^ mask) for i in range(count)])]
    unnamed x13 -> x0, local copies, waits for them, and re-layouts: 5.04 us -> none
    ppermute x2, waiting for transfers between devices: 0.57 us -> 4.88 us  [butterfly(): return lax.ppermute(x, ('grp', 'dev'), pairs)]
    add x1 -> x0, other arithmetic: 0.67 us -> none  [step(): item_grad = item_mine + item_back.astype(F32)]
    pallas_call x6 -> x7, Pallas kernels: 7.24 us -> 6.75 us  [call(): pl.pallas_call(kernel, out_shape=shapes, in_specs=specs or [vmem] * len(a...]
  transfers between devices with their start and end apart: 16 -> 16, of which waited for: 6 -> 7; matrix products, arithmetic and copies ran while one was open for 3% -> 0% of each run, Pallas kernels for 13% -> 12%
where the time goes in v3:
time: 44.2 us; the launch traced here: 44 us
  starting transfers between devices  18.5 us (42%)
  waiting for transfers between devices  17.1 us (39%)
  Pallas kernels  6.75 us (15%)
  other arithmetic  0.98 us (2%)
  between operations  0.73 us (2%)
    ppermute x14, starting transfers between devices, swap(): return lax.ppermute(x, axis, [(i, i ^ mask) for i in range(count)])  15.3 us
    ppermute x14, waiting for transfers between devices, swap(): return lax.ppermute(x, axis, [(i, i ^ mask) for i in range(count)])  12.2 us
    pallas_call x7, Pallas kernels, call(): pl.pallas_call(kernel, out_shape=shapes, in_specs=specs or [vmem] * len(a...  6.75 us
    ppermute x2, waiting for transfers between devices, butterfly(): return lax.ppermute(x, ('grp', 'dev'), pairs)  4.88 us
    ppermute x2, starting transfers between devices, butterfly(): return lax.ppermute(x, ('grp', 'dev'), pairs)  3.14 us
  transfers between devices with their start and end apart: 16, of which 7 were waited for; matrix products, arithmetic and copies ran while one was open for 0% of the time, Pallas kernels for 12%

profile of v3, /device:TPU:0, one launch (start us, length us, event | category | flops | bytes accessed | tf_op | source)
XLA Modules:
  0.0 44.0 jit_solution(10835361978722916743)
XLA Ops:
  0.6 0.6 %collective-permute-start.4 = (bf16[512,256]{1,0:T(8,128)(2,1)}, bf16[512,256]{1,0:T(8,128)(2,1)S(1)}, u32[]{:S(2)}, u32[]{:S(2)}) collective-permute-start(bf16[512,256]{1,0:T(8,128)(2,1)} %neg_hbm.1), channel_id=1, source_target_pairs={{0,1},{1,0},{2,3},{3,2},{4,5},{5,4},{6,7},{7,6},{8,9},{9,8},{10,11... | collective-permute-start | bytes 786440 | tf_op jit(solution)/shard_map/ppermute | solution.py:20
  1.2 0.1 collective-permute-start.3
  1.3 0.4 collective-permute-start.5
  1.7 2.6 %collective-permute-start = (bf16[128,256]{1,0:T(8,128)(2,1)}, bf16[128,256]{1,0:T(8,128)(2,1)S(1)}, u32[]{:S(2)}, u32[]{:S(2)}) collective-permute-start(bf16[128,256]{1,0:T(8,128)(2,1)} %q_hbm.1), channel_id=1, source_target_pairs={{0,2},{1,3},{2,0},{3,1},{4,6},{5,7},{6,4},{7,5},{8,10},{9,11},{10,... | collective-permute-start | bytes 196616 | tf_op jit(solution)/shard_map/ppermute | solution.py:20
  4.3 2.5 %collective-permute-start.2 = (bf16[128,256]{1,0:T(8,128)(2,1)}, bf16[128,256]{1,0:T(8,128)(2,1)S(1)}, u32[]{:S(2)}, u32[]{:S(2)}) collective-permute-start(bf16[128,256]{1,0:T(8,128)(2,1)} %q_hbm.1), channel_id=1, source_target_pairs={{0,6},{1,7},{2,4},{3,5},{4,2},{5,3},{6,0},{7,1},{8,14},{9,15},{10,... | collective-permute-start | bytes 196616 | tf_op jit(solution)/shard_map/ppermute | solution.py:20
  6.8 0.1 collective-permute-start.1
  6.9 2.7 %shard_map.93 = (bf16[128,256]{1,0:T(8,128)(2,1)S(1)}, bf16[128,256]{1,0:T(8,128)(2,1)S(1)}, bf16[512,256]{1,0:T(8,128)(2,1)S(1)}, f32[128,128]{1,0:T(8,128)S(1)}) custom-call(s32[1024]{0:T(1024)} %ids_ref.1, f32[2048,128]{1,0:T(8,128)} %bitcast.5, bf16[128,256]{1,0:T(8,128)(2,1)} %q_hbm.1, bf16[128,256]{1,0:T(8,128)(2,1)} %it_hbm.1, ...), custom_call_target="tpu_custom_call" | custom-call | flops 16384 | tf_op jit(solution)/shard_map/pallas_call | solution.py:242
  9.7 0.6 %shard_map.94 = (f32[3,128]{1,0:T(4,128)S(1)}, f32[1280,128]{1,0:T(8,128)S(1)}, bf16[256,1280]{1,0:T(8,128)(2,1)S(1)}, f32[128,128]{1,0:T(8,128)S(1)}) custom-call(bf16[128,256]{1,0:T(8,128)(2,1)S(1)} %get-tuple-element.34.q_ref.r_0_, bf16[128,256]{1,0:T(8,128)(2,1)S(1)} %get-tuple-element.35.it_o.r_3_, ...), custom_call_target="tpu_custom_call" | custom-call | flops 83886080 | tf_op jit(solution)/shard_map/pallas_call | solution.py:242
  10.3 1.0 %collective-permute-done.2.r_2_.r_3_ = bf16[128,256]{1,0:T(8,128)(2,1)S(1)} collective-permute-done((bf16[128,256]{1,0:T(8,128)(2,1)}, bf16[128,256]{1,0:T(8,128)(2,1)S(1)}, u32[]{:S(2)}, u32[]{:S(2)}) %collective-permute-start.2) | collective-permute-done | bytes 65568 | tf_op jit(solution)/shard_map/ppermute | solution.py:20
  11.3 2.5 %collective-permute-done.1.r_1_.r_2_ = bf16[128,256]{1,0:T(8,128)(2,1)S(1)} collective-permute-done((bf16[128,256]{1,0:T(8,128)(2,1)}, bf16[128,256]{1,0:T(8,128)(2,1)S(1)}, u32[]{:S(2)}, u32[]{:S(2)}) %collective-permute-start.1) | collective-permute-done | bytes 65568 | tf_op jit(solution)/shard_map/ppermute | solution.py:20
  13.8 1.0 %shard_map.95 = (f32[4,128]{1,0:T(4,128)S(1)}, f32[4,128]{1,0:T(4,128)S(1)}, bf16[16,128]{1,0:T(8,128)(2,1)S(1)}, f32[1280,128]{1,0:T(8,128)S(1)}, f32[1280,128]{1,0:T(8,128)S(1)}, /*index=5*/f32[1280,128]{1,0:T(8,128)S(1)}) custom-call(bf16[128,256]{1,0:T(8,128)(2,1)S(1)} %collective-permute-done.r_0_.r_1_, ...), custom_call_target="tpu_custom_call" | custom-call | flops 251658240 | tf_op jit(solution)/shard_map/pallas_call | solution.py:242
  14.8 2.8 %collective-permute-start.8 = (bf16[16,128]{1,0:T(8,128)(2,1)S(1)}, bf16[16,128]{1,0:T(8,128)(2,1)S(1)}, u32[]{:S(2)}, u32[]{:S(2)}) collective-permute-start(bf16[16,128]{1,0:T(8,128)(2,1)S(1)} %get-tuple-element.46), channel_id=1, source_target_pairs={{0,6},{1,7},{2,4},{3,5},{4,2},{5,3},{6,0},{7,1},{8,14},{9,15},{10,... | collective-permute-start | bytes 12296 | tf_op jit(solution)/shard_map/ppermute | solution.py:20
  17.6 1.7 %collective-permute-start.6 = (bf16[16,128]{1,0:T(8,128)(2,1)S(1)}, bf16[16,128]{1,0:T(8,128)(2,1)S(1)}, u32[]{:S(2)}, u32[]{:S(2)}) collective-permute-start(bf16[16,128]{1,0:T(8,128)(2,1)S(1)} %get-tuple-element.46), channel_id=1, source_target_pairs={{0,2},{1,3},{2,0},{3,1},{4,6},{5,7},{6,4},{7,5},{8,10},{9,11},{10,... | collective-permute-start | bytes 12296 | tf_op jit(solution)/shard_map/ppermute | solution.py:20
  19.3 1.0 %collective-permute-done.8.r_13_ = bf16[16,128]{1,0:T(8,128)(2,1)S(1)} collective-permute-done((bf16[16,128]{1,0:T(8,128)(2,1)S(1)}, bf16[16,128]{1,0:T(8,128)(2,1)S(1)}, u32[]{:S(2)}, u32[]{:S(2)}) %collective-permute-start.8) | collective-permute-done | bytes 4128 | tf_op jit(solution)/shard_map/ppermute | solution.py:20
  20.3 1.8 %collective-permute-done.7.r_12_ = bf16[16,128]{1,0:T(8,128)(2,1)S(1)} collective-permute-done((bf16[16,128]{1,0:T(8,128)(2,1)S(1)}, bf16[16,128]{1,0:T(8,128)(2,1)S(1)}, u32[]{:S(2)}, u32[]{:S(2)}) %collective-permute-start.7) | collective-permute-done | bytes 4128 | tf_op jit(solution)/shard_map/ppermute | solution.py:20
  22.1 0.4 shard_map.96
  22.4 0.1 collective-permute-start.9
  22.5 0.3 shard_map.97
  22.8 1.2 %collective-permute-done.9 = bf16[512,256]{1,0:T(8,128)(2,1)S(1)} collective-permute-done((bf16[512,256]{1,0:T(8,128)(2,1)S(1)}, bf16[512,256]{1,0:T(8,128)(2,1)S(1)}, u32[]{:S(2)}, u32[]{:S(2)}) %collective-permute-start.9) | collective-permute-done | bytes 262176 | tf_op jit(solution)/shard_map/ppermute | solution.py:20
  24.0 0.1 add_convert_fusion.1.r_5_
  24.1 1.6 %collective-permute-start.14 = (bf16[512,256]{1,0:T(8,128)(2,1)S(1)}, bf16[512,256]{1,0:T(8,128)(2,1)S(1)}, u32[]{:S(2)}, u32[]{:S(2)}) collective-permute-start(bf16[512,256]{1,0:T(8,128)(2,1)S(1)} %add_convert_fusion.1.r_5_), channel_id=1, source_target_pairs={{0,8},{1,17},{2,10},{3,19},{4,12},{5,21},{6,14},{7,23},{8,0},{9,25... | collective-permute-start | bytes 786440 | tf_op jit(solution)/shard_map/ppermute | solution.py:259
  25.7 4.9 %collective-permute-done.14 = bf16[512,256]{1,0:T(8,128)(2,1)S(1)} collective-permute-done((bf16[512,256]{1,0:T(8,128)(2,1)S(1)}, bf16[512,256]{1,0:T(8,128)(2,1)S(1)}, u32[]{:S(2)}, u32[]{:S(2)}) %collective-permute-start.14) | collective-permute-done | bytes 262176 | tf_op jit(solution)/shard_map/ppermute | solution.py:259
  30.5 0.1 add_convert_fusion
  30.6 1.6 %collective-permute-start.15 = (bf16[512,256]{1,0:T(8,128)(2,1)S(1)}, bf16[512,256]{1,0:T(8,128)(2,1)S(1)}, u32[]{:S(2)}, u32[]{:S(2)}) collective-permute-start(bf16[512,256]{1,0:T(8,128)(2,1)S(1)} %add_convert_fusion), channel_id=1, source_target_pairs={{0,16},{1,9},{2,18},{3,11},{4,20},{5,13},{6,22},{7,15},{8,24},{9,1... | collective-permute-start | bytes 786440 | tf_op jit(solution)/shard_map/ppermute | solution.py:259
  32.2 0.9 %shard_map.98 = (f32[128,256]{1,0:T(8,128)S(1)}, bf16[128,256]{1,0:T(8,128)(2,1)S(1)}, f32[256,128]{1,0:T(8,128)S(1)}, bf16[256,128]{1,0:T(8,128)(2,1)S(1)}, bf1...) custom-call(bf16[512,256]{1,0:T(8,128)(2,1)S(1)} %get-tuple-element.48.r_0_, ...), custom_call_target="tpu_custom_call" | custom-call | flops 671088640 | tf_op jit(solution)/shard_map/pallas_call | solution.py:242
  33.1 0.1 collective-permute-start.10
  33.2 0.9 %collective-permute-start.11 = (bf16[256,128]{1,0:T(8,128)(2,1)S(1)}, bf16[256,128]{1,0:T(8,128)(2,1)S(1)}, u32[]{:S(2)}, u32[]{:S(2)}) collective-permute-start(bf16[256,128]{1,0:T(8,128)(2,1)S(1)} %get-tuple-element.58), channel_id=1, source_target_pairs={{0,2},{1,3},{2,0},{3,1},{4,6},{5,7},{6,4},{7,5},{8,10},{9,11},{10,... | collective-permute-start | bytes 196616 | tf_op jit(solution)/shard_map/ppermute | solution.py:20
  34.1 1.3 %collective-permute-start.12 = (bf16[256,128]{1,0:T(8,128)(2,1)S(1)}, bf16[256,128]{1,0:T(8,128)(2,1)S(1)}, u32[]{:S(2)}, u32[]{:S(2)}) collective-permute-start(bf16[256,128]{1,0:T(8,128)(2,1)S(1)} %get-tuple-element.59), channel_id=1, source_target_pairs={{0,4},{1,5},{2,6},{3,7},{4,0},{5,1},{6,2},{7,3},{8,12},{9,13},{10,... | collective-permute-start | bytes 196616 | tf_op jit(solution)/shard_map/ppermute | solution.py:20
  35.4 2.3 %collective-permute-start.13 = (bf16[256,128]{1,0:T(8,128)(2,1)S(1)}, bf16[256,128]{1,0:T(8,128)(2,1)S(1)}, u32[]{:S(2)}, u32[]{:S(2)}) collective-permute-start(bf16[256,128]{1,0:T(8,128)(2,1)S(1)} %get-tuple-element.60), channel_id=1, source_target_pairs={{0,6},{1,7},{2,4},{3,5},{4,2},{5,3},{6,0},{7,1},{8,14},{9,15},{10,... | collective-permute-start | bytes 196616 | tf_op jit(solution)/shard_map/ppermute | solution.py:20
  37.7 4.7 %collective-permute-done.12.refs_1_ = bf16[256,128]{1,0:T(8,128)(2,1)S(1)} collective-permute-done((bf16[256,128]{1,0:T(8,128)(2,1)S(1)}, bf16[256,128]{1,0:T(8,128)(2,1)S(1)}, u32[]{:S(2)}, u32[]{:S(2)}) %collective-permute-start.12) | collective-permute-done | bytes 65568 | tf_op jit(solution)/shard_map/ppermute | solution.py:20
  42.4 0.8 %shard_map.99 = (f32[1,128]{1,0:T(1,128)}, f32[128,256]{1,0:T(8,128)}, f32[128,256]{1,0:T(8,128)}) custom-call(f32[1,128]{1,0:T(1,128)S(1)} %get-tuple-element.47.loss_in, f32[128,256]{1,0:T(8,128)S(1)} %get-tuple-element.55.mine_ref, bf16[128,256]{1,0:T(8,128)(2,1)S(1)} %collective-permute-done.10.back_ref, f32[256,128]{1,0:T(8,128)S(1)} %get-tuple-element.57.own_ref, ...), custom_call_target="tpu_custom_call" | custom-call | flops 131072 | tf_op jit(solution)/shard_map/pallas_call | solution.py:242
  43.2 0.8 %convert_add_fusion = f32[512,256]{1,0:T(8,128)} fusion(bf16[512,256]{1,0:T(8,128)(2,1)S(1)} %collective-permute-done.15, bf16[512,256]{1,0:T(8,128)(2,1)S(1)} %add_convert_fusion), kind=kLoop, calls=%fused_computation | loop fusion | flops 393216 | bytes 1048576 | tf_op jit(solution)/shard_map/add | solution.py:364
  (10 shorter events, 0.1 us)
Async XLA Ops:
  0.6 9.1 %collective-permute-start.4 = (bf16[512,256]{1,0:T(8,128)(2,1)}, bf16[512,256]{1,0:T(8,128)(2,1)S(1)}, u32[]{:S(2)}, u32[]{:S(2)}) collective-permute-start(bf16[512,256]{1,0:T(8,128)(2,1)} %neg_hbm.1), channel_id=1, source_target_pairs={{0,1},{1,0},{2,3},{3,2},{4,5},{5,4},{6,7},{7,6},{8,9},{9,8},{10,11... | collective-permute-start | bytes 786440 | tf_op jit(solution)/shard_map/ppermute | solution.py:20
  1.2 8.5 %collective-permute-start.3 = (bf16[128,256]{1,0:T(8,128)(2,1)}, bf16[128,256]{1,0:T(8,128)(2,1)S(1)}, u32[]{:S(2)}, u32[]{:S(2)}) collective-permute-start(bf16[128,256]{1,0:T(8,128)(2,1)} %it_hbm.1), channel_id=1, source_target_pairs={{0,1},{1,0},{2,3},{3,2},{4,5},{5,4},{6,7},{7,6},{8,9},{9,8},{10,11... | collective-permute-start | bytes 196616 | tf_op jit(solution)/shard_map/ppermute | solution.py:20
  1.3 5.5 %collective-permute-start.5 = (f32[512]{0:T(512)}, f32[512]{0:T(512)S(1)}, u32[]{:S(2)}, u32[]{:S(2)}) collective-permute-start(f32[512]{0:T(512)} %param.10), channel_id=1, source_target_pairs={{0,1},{1,0},{2,3},{3,2},{4,5},{5,4},{6,7},{7,6},{8,9},{9,8},{10,11... | collective-permute-start | bytes 6152 | tf_op jit(solution)/shard_map/ppermute | solution.py:20
  1.7 8.6 %collective-permute-start = (bf16[128,256]{1,0:T(8,128)(2,1)}, bf16[128,256]{1,0:T(8,128)(2,1)S(1)}, u32[]{:S(2)}, u32[]{:S(2)}) collective-permute-start(bf16[128,256]{1,0:T(8,128)(2,1)} %q_hbm.1), channel_id=1, source_target_pairs={{0,2},{1,3},{2,0},{3,1},{4,6},{5,7},{6,4},{7,5},{8,10},{9,11},{10,... | collective-permute-start | bytes 196616 | tf_op jit(solution)/shard_map/ppermute | solution.py:20
  4.3 6.9 %collective-permute-start.2 = (bf16[128,256]{1,0:T(8,128)(2,1)}, bf16[128,256]{1,0:T(8,128)(2,1)S(1)}, u32[]{:S(2)}, u32[]{:S(2)}) collective-permute-start(bf16[128,256]{1,0:T(8,128)(2,1)} %q_hbm.1), channel_id=1, source_target_pairs={{0,6},{1,7},{2,4},{3,5},{4,2},{5,3},{6,0},{7,1},{8,14},{9,15},{10,... | collective-permute-start | bytes 196616 | tf_op jit(solution)/shard_map/ppermute | solution.py:20
  6.8 7.0 %collective-permute-start.1 = (bf16[128,256]{1,0:T(8,128)(2,1)}, bf16[128,256]{1,0:T(8,128)(2,1)S(1)}, u32[]{:S(2)}, u32[]{:S(2)}) collective-permute-start(bf16[128,256]{1,0:T(8,128)(2,1)} %q_hbm.1), channel_id=1, source_target_pairs={{0,4},{1,5},{2,6},{3,7},{4,0},{5,1},{6,2},{7,3},{8,12},{9,13},{10,... | collective-permute-start | bytes 196616 | tf_op jit(solution)/shard_map/ppermute | solution.py:20
  14.8 5.5 %collective-permute-start.8 = (bf16[16,128]{1,0:T(8,128)(2,1)S(1)}, bf16[16,128]{1,0:T(8,128)(2,1)S(1)}, u32[]{:S(2)}, u32[]{:S(2)}) collective-permute-start(bf16[16,128]{1,0:T(8,128)(2,1)S(1)} %get-tuple-element.46), channel_id=1, source_target_pairs={{0,6},{1,7},{2,4},{3,5},{4,2},{5,3},{6,0},{7,1},{8,14},{9,15},{10,... | collective-permute-start | bytes 12296 | tf_op jit(solution)/shard_map/ppermute | solution.py:20
  17.6 4.5 %collective-permute-start.7 = (bf16[16,128]{1,0:T(8,128)(2,1)S(1)}, bf16[16,128]{1,0:T(8,128)(2,1)S(1)}, u32[]{:S(2)}, u32[]{:S(2)}) collective-permute-start(bf16[16,128]{1,0:T(8,128)(2,1)S(1)} %get-tuple-element.46), channel_id=1, source_target_pairs={{0,4},{1,5},{2,6},{3,7},{4,0},{5,1},{6,2},{7,3},{8,12},{9,13},{10,... | collective-permute-start | bytes 12296 | tf_op jit(solution)/shard_map/ppermute | solution.py:20
  17.6 4.5 %collective-permute-start.6 = (bf16[16,128]{1,0:T(8,128)(2,1)S(1)}, bf16[16,128]{1,0:T(8,128)(2,1)S(1)}, u32[]{:S(2)}, u32[]{:S(2)}) collective-permute-start(bf16[16,128]{1,0:T(8,128)(2,1)S(1)} %get-tuple-element.46), channel_id=1, source_target_pairs={{0,2},{1,3},{2,0},{3,1},{4,6},{5,7},{6,4},{7,5},{8,10},{9,11},{10,... | collective-permute-start | bytes 12296 | tf_op jit(solution)/shard_map/ppermute | solution.py:20
  22.4 1.6 %collective-permute-start.9 = (bf16[512,256]{1,0:T(8,128)(2,1)S(1)}, bf16[512,256]{1,0:T(8,128)(2,1)S(1)}, u32[]{:S(2)}, u32[]{:S(2)}) collective-permute-start(bf16[512,256]{1,0:T(8,128)(2,1)S(1)} %get-tuple-element.54), channel_id=1, source_target_pairs={{0,1},{1,0},{2,3},{3,2},{4,5},{5,4},{6,7},{7,6},{8,9},{9,8},{10,11... | collective-permute-start | bytes 786440 | tf_op jit(solution)/shard_map/ppermute | solution.py:20
  24.1 6.4 %collective-permute-start.14 = (bf16[512,256]{1,0:T(8,128)(2,1)S(1)}, bf16[512,256]{1,0:T(8,128)(2,1)S(1)}, u32[]{:S(2)}, u32[]{:S(2)}) collective-permute-start(bf16[512,256]{1,0:T(8,128)(2,1)S(1)} %add_convert_fusion.1.r_5_), channel_id=1, source_target_pairs={{0,8},{1,17},{2,10},{3,19},{4,12},{5,21},{6,14},{7,23},{8,0},{9,25... | collective-permute-start | bytes 786440 | tf_op jit(solution)/shard_map/ppermute | solution.py:259
  30.6 12.6 %collective-permute-start.15 = (bf16[512,256]{1,0:T(8,128)(2,1)S(1)}, bf16[512,256]{1,0:T(8,128)(2,1)S(1)}, u32[]{:S(2)}, u32[]{:S(2)}) collective-permute-start(bf16[512,256]{1,0:T(8,128)(2,1)S(1)} %add_convert_fusion), channel_id=1, source_target_pairs={{0,16},{1,9},{2,18},{3,11},{4,20},{5,13},{6,22},{7,15},{8,24},{9,1... | collective-permute-start | bytes 786440 | tf_op jit(solution)/shard_map/ppermute | solution.py:259
  33.1 4.5 %collective-permute-start.10 = (bf16[128,256]{1,0:T(8,128)(2,1)S(1)}, bf16[128,256]{1,0:T(8,128)(2,1)S(1)}, u32[]{:S(2)}, u32[]{:S(2)}) collective-permute-start(bf16[128,256]{1,0:T(8,128)(2,1)S(1)} %get-tuple-element.56), channel_id=1, source_target_pairs={{0,1},{1,0},{2,3},{3,2},{4,5},{5,4},{6,7},{7,6},{8,9},{9,8},{10,11... | collective-permute-start | bytes 196616 | tf_op jit(solution)/shard_map/ppermute | solution.py:20
  33.2 4.5 %collective-permute-start.11 = (bf16[256,128]{1,0:T(8,128)(2,1)S(1)}, bf16[256,128]{1,0:T(8,128)(2,1)S(1)}, u32[]{:S(2)}, u32[]{:S(2)}) collective-permute-start(bf16[256,128]{1,0:T(8,128)(2,1)S(1)} %get-tuple-element.58), channel_id=1, source_target_pairs={{0,2},{1,3},{2,0},{3,1},{4,6},{5,7},{6,4},{7,5},{8,10},{9,11},{10,... | collective-permute-start | bytes 196616 | tf_op jit(solution)/shard_map/ppermute | solution.py:20
  34.1 8.3 %collective-permute-start.12 = (bf16[256,128]{1,0:T(8,128)(2,1)S(1)}, bf16[256,128]{1,0:T(8,128)(2,1)S(1)}, u32[]{:S(2)}, u32[]{:S(2)}) collective-permute-start(bf16[256,128]{1,0:T(8,128)(2,1)S(1)} %get-tuple-element.59), channel_id=1, source_target_pairs={{0,4},{1,5},{2,6},{3,7},{4,0},{5,1},{6,2},{7,3},{8,12},{9,13},{10,... | collective-permute-start | bytes 196616 | tf_op jit(solution)/shard_map/ppermute | solution.py:20
  35.4 7.0 %collective-permute-start.13 = (bf16[256,128]{1,0:T(8,128)(2,1)S(1)}, bf16[256,128]{1,0:T(8,128)(2,1)S(1)}, u32[]{:S(2)}, u32[]{:S(2)}) collective-permute-start(bf16[256,128]{1,0:T(8,128)(2,1)S(1)} %get-tuple-element.60), channel_id=1, source_target_pairs={{0,6},{1,7},{2,4},{3,5},{4,2},{5,3},{6,0},{7,1},{8,14},{9,15},{10,... | collective-permute-start | bytes 196616 | tf_op jit(solution)/shard_map/ppermute | solution.py:20

commit v4 on v3

--- a/solution.py
+++ b/solution.py
@@ -44,39 +44,35 @@
     return [(ref, first) for ref in refs for first in range(0, ref.shape[0], rows)]
 
 
-def prepare_kernel(ids_ref, table_hbm, q_hbm, it_hbm, neg_hbm, lq_hbm, *refs):
-    q_ref, it_ref, neg_ref, cols_ref, table, lq, picked, sems = refs
-    copies = [
-        pltpu.make_async_copy(src, dst, sems.at[i])
-        for i, (src, dst) in enumerate(
-            [(table_hbm, table), (lq_hbm, lq), (q_hbm, q_ref), (it_hbm, it_ref), (neg_hbm, neg_ref)]
-        )
+def prepare_kernel(chunks, ids_hbm, table_hbm, q_hbm, it_hbm, neg_hbm, lq_hbm, *refs):
+    q_ref, it_ref, neg_ref, cols_ref, ids, table, lq, picked, sems = refs
+    part = table.shape[0] // chunks
+    moves = [(ids_hbm, ids), (lq_hbm, lq)]
+    moves += [
+        (table_hbm.at[pl.ds(i * part, part), :], table.at[pl.ds(i * part, part), :]) for i in range(chunks)
     ]
+    moves += [(q_hbm, q_ref), (it_hbm, it_ref), (neg_hbm, neg_ref)]
+    copies = [pltpu.make_async_copy(src, dst, sems.at[i]) for i, (src, dst) in enumerate(moves)]
     for c in copies:
         c.start()
-    copies[0].wait()
-    copies[1].wait()
+    for c in copies[: 2 + chunks]:
+        c.wait()
     rows, _ = q_ref.shape
     dev = lax.axis_index("dev")
     lane = lax.broadcasted_iota(jnp.int32, (1, LANES), 1)
     for half, owner in enumerate((dev, dev ^ 1)):
         start = owner * rows
-
-        def pick(i, carry, half=half, start=start):
-            for t in range(8):
-                j = i * 8 + t
-                item = ids_ref[start + j]
-                row = table[pl.ds(lax.shift_right_logical(item, 7), 1), :]
-                picked[pl.ds(half * rows + j, 1), :] = jnp.where(lane == (item & (LANES - 1)), row, 0.0)
-            return carry
-
-        lax.fori_loop(0, rows // 8, pick, 0)
+        for j in range(rows):
+            item = ids[start + j]
+            row = table[pl.ds(lax.shift_right_logical(item, 7), 1), :]
+            at = half * rows + j
+            picked[at : at + 1, :] = jnp.where(lane == (item & (LANES - 1)), row, 0.0)
     for half in range(2):
-        part = picked[half * rows : (half + 1) * rows, :]
-        cols_ref[:, half : half + 1] = jnp.sum(part, axis=1, keepdims=True)
+        run = picked[half * rows : (half + 1) * rows, :]
+        cols_ref[:, half : half + 1] = jnp.sum(run, axis=1, keepdims=True)
     own = lq.shape[0]
     cols_ref[:, 2 : 2 + own] = pad_rows([lq[...]], 8).T[:, :own]
-    for c in copies[2:]:
+    for c in copies[2 + chunks :]:
         c.wait()
 
 
@@ -98,7 +94,8 @@
         e_ref[j * rows : (j + 1) * rows, :] = e
         here = fold(e, jnp.sum)
         total = here if total is None else total + here
-    return row_max, row_max + jnp.log(jnp.sum(total, axis=0, keepdims=True)), matched
+    row_sum = jnp.sum(total, axis=0, keepdims=True)
+    return row_max, row_max + jnp.log(row_sum), matched, row_sum
 
 
 def own_mask(rows):
@@ -120,25 +117,54 @@
     cols_ref[:, :negs] = pad_rows([lq_p[...]], 8).T[:, :negs]
     runs = runs_of((it_o, it_p, neg_o, neg_p), rows)
     cols = candidate_cols(cols_own, cols_ref, negs)
-    stat_ref[0:1, :], stat_ref[1:2, :], stat_ref[2:3, :] = first_pass(runs, cols, q_ref[...], e_ref, True)
+    top, lse, matched, _ = first_pass(runs, cols, q_ref[...], e_ref, True)
+    stat_ref[0:1, :] = top
+    stat_ref[1:2, :] = lse
+    stat_ref[2:3, :] = matched
     for j, (ref, first) in enumerate(runs):
         ct_ref[:, j * rows : (j + 1) * rows] = ref[first : first + rows, :].T
 
 
-def other_blocks_kernel(n, *refs):
-    q_refs, refs = refs[: n - 1], refs[n - 1 :]
-    c_refs, (cols_own, cols_par, stat0_ref), refs = refs[:4], refs[4:7], refs[7:]
-    max_ref, lse_ref, msg_ref, e_refs = refs[0], refs[1], refs[2], refs[3:]
+def other_blocks_kernel(count, near, *refs):
+    q_refs, refs = refs[:count], refs[count:]
+    c_refs, (cols_own, cols_par), refs = refs[:4], refs[4:6], refs[6:]
     rows, _ = q_refs[0].shape
     runs = runs_of(c_refs, rows)
     cols = candidate_cols(cols_own, cols_par, c_refs[2].shape[0] // rows)
-    max_ref[0:1, :] = stat0_ref[0:1, :]
-    lse_ref[0:1, :] = stat0_ref[1:2, :]
-    for k in range(1, n):
-        top, lse, _ = first_pass(runs, cols, q_refs[k - 1][...], e_refs[k - 1], False)
+    if near is not None:
+        ct_ref, refs = refs[0], refs[1:]
+    stat_ref, e_refs, rest = refs[0], refs[1 : 1 + count], refs[1 + count :]
+    for i in range(count):
+        top, lse, _, total = first_pass(runs, cols, q_refs[i][...], e_refs[i], False)
+        stat_ref[2 * i : 2 * i + 1, :] = top
+        stat_ref[2 * i + 1 : 2 * i + 2, :] = lse
+        if i == near:
+            u = jnp.dot(ct_ref[...], e_refs[i][...].astype(BF16), preferred_element_type=F32)
+            rest[0][...] = (u * (1.0 / total)).astype(BF16)
+
+
+def last_block_kernel(n, order, q_ref, *refs):
+    c_refs, (cols_own, cols_par, stat0, stat_rest, near_u), refs = refs[:4], refs[4:9], refs[9:]
+    max_ref, lse_ref, msg_ref, near_ref, e_ref = refs
+    rows, _ = q_ref.shape
+    runs = runs_of(c_refs, rows)
+    cols = candidate_cols(cols_own, cols_par, c_refs[2].shape[0] // rows)
+    last = first_pass(runs, cols, q_ref[...], e_ref, False)
+    for k in range(n):
+        if k == 0:
+            top, lse = stat0[0:1, :], stat0[1:2, :]
+        elif k == order[-1]:
+            top, lse = last[:2]
+        else:
+            i = order.index(k)
+            top, lse = stat_rest[2 * i : 2 * i + 1, :], stat_rest[2 * i + 1 : 2 * i + 2, :]
         max_ref[k : k + 1, :] = top
         lse_ref[k : k + 1, :] = lse
-    msg_ref[...] = pad_rows(split3(lse_ref[...]), 16)
+    width = near_u.shape[0]
+    near_ref[:width, :] = near_u[...]
+    msg = pad_rows(split3(lse_ref[...]), 16)
+    msg_ref[...] = msg
+    near_ref[width:, :] = msg
 
 
 def second_pass(n, e_refs, offset, q_all, weight_ref, mask_first, p_ref, emit):
@@ -154,16 +180,16 @@
         emit(j, jnp.dot(p_ref[run, :], q_all[...], preferred_element_type=F32))
 
 
-def partner_kernel(n, offset, *refs):
+def partner_kernel(n, offset, width, *refs):
     q_refs, e_refs, refs = refs[:n], refs[n : 2 * n], refs[2 * n :]
     max_ref, lse_ref, stat0_ref, refs = refs[0], refs[1], refs[2], refs[3:]
-    got_refs, (out_ref, p_ref, weight_ref, loss_ref, q_all) = refs[: n - 1], refs[n - 1 :]
+    got_refs, (out_ref, p_ref, weight_ref, loss_ref, near_ref, q_all) = refs[: n - 1], refs[n - 1 :]
     rows, _ = q_refs[0].shape
     for k in range(n):
         q_all[k * rows : (k + 1) * rows, :] = q_refs[k][...]
     totals = [lse_ref[...]]
-    for ref in got_refs:
-        got = ref[...].astype(F32)
+    for k, ref in enumerate(got_refs):
+        got = (ref[width:, :] if k == 0 else ref[...]).astype(F32)
         totals.append(got[:n] + got[n : 2 * n] + got[2 * n : 3 * n])
     for b in range(n):
         parts = [totals[k][k ^ b : (k ^ b) + 1, :] for k in range(n)]
@@ -177,6 +203,7 @@
         weight_ref[b : b + 1, :] = logit_scale * jnp.exp(max_ref[b : b + 1, :] - norm)
         if b == 0:
             loss_ref[...] = norm - stat0_ref[2:3, :]
+            near_ref[...] = logit_scale * jnp.exp(totals[1][1:2, :] - norm)
 
     def emit(j, g):
         out_ref[j * rows : (j + 1) * rows, :] = g.astype(BF16)
@@ -184,46 +211,40 @@
     second_pass(n, e_refs, offset, q_all, weight_ref, False, p_ref, emit)
 
 
-def own_kernel(n, offset, q_all, weight_ref, *refs):
-    e_refs, (out_ref, p_ref) = refs[:n], refs[n:]
+def own_kernel(n, q_all, weight_ref, *refs):
+    e_refs, (out_ref, p_ref, mine_ref, theirs_ref, p_items) = refs[:n], refs[n:]
     rows = q_all.shape[0] // n
 
     def emit(j, g):
         out_ref[j * rows : (j + 1) * rows, :] = g
 
-    second_pass(n, e_refs, offset, q_all, weight_ref, False, p_ref, emit)
-
-
-def items_kernel(n, q_all, weight_ref, ct_ref, p_own, p_par, _, *refs):
-    e_refs, refs = refs[:n], refs[n:]
-    (mine_ref, theirs_ref, own_ref), refs = refs[:3], refs[3:]
-    msg_refs, (p_ref,) = refs[: n - 1], refs[n - 1 :]
-    rows = q_all.shape[0] // n
-    negs = p_own.shape[0]
-
-    def emit(j, g):
+    def emit_item(j, g):
         if j == 0:
             mine_ref[...] = g
         else:
             theirs_ref[...] = g.astype(BF16)
 
-    second_pass(n, e_refs, 0, q_all, weight_ref, True, p_ref, emit)
-    for k in range(n):
+    second_pass(n, e_refs, 2 * rows, q_all, weight_ref, False, p_ref, emit)
+    second_pass(n, e_refs, 0, q_all, weight_ref, True, p_items, emit_item)
+
+
+def partial_kernel(blocks, ct_ref, p_items, p_own, p_par, *out_refs):
+    rows = out_refs[0].shape[1]
+    item_rows, negs = p_items.shape[0], p_own.shape[0]
+    for k, out_ref in zip(blocks, out_refs):
         part = slice(k * rows, (k + 1) * rows)
-        u = jnp.dot(ct_ref[:, : 2 * rows], p_ref[:, part], preferred_element_type=F32)
-        u += jnp.dot(ct_ref[:, 2 * rows : 2 * rows + negs], p_own[:, part], preferred_element_type=F32)
-        u += jnp.dot(ct_ref[:, 2 * rows + negs :], p_par[:, part], preferred_element_type=F32)
-        if k == 0:
-            own_ref[...] = u
-        else:
-            msg_refs[k - 1][...] = u.astype(BF16)
-
-
-def outputs_kernel(loss_in, mine_ref, back_ref, own_ref, *refs):
+        u = jnp.dot(ct_ref[:, :item_rows], p_items[:, part], preferred_element_type=F32)
+        u += jnp.dot(ct_ref[:, item_rows : item_rows + negs], p_own[:, part], preferred_element_type=F32)
+        u += jnp.dot(ct_ref[:, item_rows + negs :], p_par[:, part], preferred_element_type=F32)
+        out_ref[...] = u.astype(out_ref.dtype)
+
+
+def outputs_kernel(loss_in, mine_ref, back_ref, own_ref, near_w, near_u, *refs):
     loss_ref, query_ref, item_ref = refs[-3:]
     loss_ref[...] = loss_in[...]
     item_ref[...] = mine_ref[...] + back_ref[...].astype(F32)
-    total = own_ref[...]
+    width = own_ref.shape[0]
+    total = own_ref[...] + near_w[...] * near_u[:width, :].astype(F32)
     for ref in refs[:-3]:
         total = total + ref[...].astype(F32)
     query_ref[...] = total.T
@@ -281,8 +302,10 @@
         hbm = pl.BlockSpec(memory_space=pl.ANY)
         table_shape = (logq_table.size // LANES, LANES)
 
+        chunks = 4 if table_shape[0] % 32 == 0 else 1
+
         q0, items, neg_embed, cols = call(
-            prepare_kernel,
+            lambda *r: prepare_kernel(chunks, *r),
             [((rows, width), BF16), ((rows, width), BF16), ((negs, width), BF16), ((rows, LANES), F32)],
             (
                 item_ids,
@@ -293,13 +316,14 @@
                 neg_logq.reshape(per_run, rows),
             ),
             [
+                pltpu.SMEM(item_ids.shape, jnp.int32),
                 pltpu.VMEM(table_shape, F32),
                 pltpu.VMEM((per_run, rows), F32),
                 pltpu.VMEM((2 * rows, LANES), F32),
-                pltpu.SemaphoreType.DMA((5,)),
+                pltpu.SemaphoreType.DMA((5 + chunks,)),
             ],
             (rows * LANES, 0),
-            [pl.BlockSpec(memory_space=pltpu.SMEM)] + [hbm] * 5,
+            [hbm] * 6,
         )
         cand_refs = (items, items_p, neg_embed, neg_p)
         stat0, e0, c_t, cols_p = call(
@@ -309,24 +333,41 @@
             (),
             (unit * cands, rows * cands),
         )
+        last = n // 2
+        order = [k for k in range(1, n) if k != last] + [last]
+        many = n - 2
+        stat_rest, *rest = call(
+            lambda *r: other_blocks_kernel(many, 0, *r),
+            [((2 * many, rows), F32)] + [((cands, rows), F32)] * many + [((width, rows), BF16)],
+            (*[others[k - 1] for k in order[:-1]], *cand_refs, cols, cols_p, c_t),
+            (),
+            (many * unit * cands, many * rows * cands),
+        )
         msg_rows = round_up(3 * n, 16)
-        tops, lse, msg, *e_rest = call(
-            lambda *r: other_blocks_kernel(n, *r),
-            [((n, rows), F32), ((n, rows), F32), ((msg_rows, rows), BF16)]
-            + [((cands, rows), F32)] * (n - 1),
-            (*others, *cand_refs, cols, cols_p, stat0),
-            (),
-            ((n - 1) * unit * cands, (n - 1) * rows * cands),
-        )
-        e = (e0, *e_rest)
-        got = [exchange(msg, k) for k in range(1, n)]
-        theirs, p_par, weight, loss, q_all = call(
-            lambda *r: partner_kernel(n, 2 * rows + negs, *r),
+        tops, lse, msg, near_msg, e_last = call(
+            lambda *r: last_block_kernel(n, order, *r),
+            [
+                ((n, rows), F32),
+                ((n, rows), F32),
+                ((msg_rows, rows), BF16),
+                ((width + msg_rows, rows), BF16),
+                ((cands, rows), F32),
+            ],
+            (others[last - 1], *cand_refs, cols, cols_p, stat0, stat_rest, rest[-1]),
+            (),
+            (unit * cands, rows * cands),
+        )
+        by_block = dict(zip(order, [*rest[:-1], e_last]))
+        e = (e0, *[by_block[k] for k in range(1, n)])
+        got = [exchange(near_msg if k == 1 else msg, k) for k in range(1, n)]
+        theirs, p_par, weight, loss, near_w, q_all = call(
+            lambda *r: partner_kernel(n, 2 * rows + negs, width, *r),
             [
                 ((negs, width), BF16),
                 ((negs, n * rows), BF16),
                 ((n, rows), F32),
                 ((1, rows), F32),
+                ((1, rows), F32),
                 ((n * rows, width), BF16),
             ],
             (q0, *others, *e, tops, lse, stat0, *got),
@@ -334,28 +375,34 @@
             (n * unit * negs, 0),
         )
         back = partner(theirs)
-        mine, p_own = call(
-            lambda *r: own_kernel(n, 2 * rows, *r),
-            [((negs, width), F32), ((negs, n * rows), BF16)],
+        mine, p_own, item_mine, item_theirs, p_items = call(
+            lambda *r: own_kernel(n, *r),
+            [
+                ((negs, width), F32),
+                ((negs, n * rows), BF16),
+                ((rows, width), F32),
+                ((rows, width), BF16),
+                ((2 * rows, n * rows), BF16),
+            ],
             (q_all, weight, *e),
             (),
-            (n * unit * negs, 0),
+            (n * unit * (negs + 2 * rows), 0),
+        )
+        blocks = [0] + list(range(2, n))
+        u_own, *u_msgs = call(
+            lambda *r: partial_kernel(blocks, *r),
+            [((width, rows), F32)] + [((width, rows), BF16)] * (n - 2),
+            (c_t, p_items, p_own, p_par),
+            (),
+            ((n - 1) * unit * cands, 0),
         )
         part = (mine + back.astype(F32)).astype(BF16)
-        item_mine, item_theirs, u_own, *u_msgs = call(
-            lambda *r: items_kernel(n, *r),
-            [((rows, width), F32), ((rows, width), BF16), ((width, rows), F32)]
-            + [((width, rows), BF16)] * (n - 1),
-            (q_all, weight, c_t, p_own, p_par, part, *e),
-            [pltpu.VMEM((2 * rows, n * rows), BF16)],
-            (2 * n * unit * cands, 0),
-        )
         item_back = partner(item_theirs)
-        u_got = [exchange(u_msgs[k - 1], k) for k in range(1, n)]
+        u_got = [exchange(u, k) for k, u in zip(blocks[1:], u_msgs)]
         loss, query_grad, item_grad = call(
             outputs_kernel,
             [shape((1, rows), F32), shape((rows, width), F32), shape((rows, width), F32)],
-            (loss, item_mine, item_back, u_own, *u_got),
+            (loss, item_mine, item_back, u_own, near_w, got[0], *u_got),
             (),
             (n * rows * width, 0),
         )

time: 44.2 us -> 42.7 us (0.966)
  starting transfers between devices: 18.5 us -> 16.2 us
  waiting for transfers between devices: 17.1 us -> 18.5 us
  Pallas kernels: 6.75 us -> 6.07 us
    ppermute x14 -> x13, starting transfers between devices: 15.3 us -> 13.1 us  [swap(): return lax.ppermute(x, axis, [(i, i ^ mask) for i in range(count)])]
    ppermute x14 -> x13, waiting for transfers between devices: 12.2 us -> 13.6 us  [swap(): return lax.ppermute(x, axis, [(i, i ^ mask) for i in range(count)])]
    pallas_call x7 -> x8, Pallas kernels: 6.75 us -> 6.07 us  [call(): pl.pallas_call(kernel, out_shape=shapes, in_specs=specs or [vmem] * len(a...]
  transfers between devices with their start and end apart: 16 -> 15, of which waited for: 7 -> 8; matrix products, arithmetic and copies ran while one was open for 0% -> 0% of each run, Pallas kernels for 12% -> 12%
where the time goes in v4:
time: 42.7 us; the launch traced here: 42.5 us
  waiting for transfers between devices  18.5 us (43%)
  starting transfers between devices  16.2 us (38%)
  Pallas kernels  6.07 us (14%)
  other arithmetic  0.98 us (2%)
  between operations  0.73 us (2%)
    ppermute x13, waiting for transfers between devices, swap(): return lax.ppermute(x, axis, [(i, i ^ mask) for i in range(count)])  13.6 us
    ppermute x13, starting transfers between devices, swap(): return lax.ppermute(x, axis, [(i, i ^ mask) for i in range(count)])  13.1 us
    pallas_call x8, Pallas kernels, call(): pl.pallas_call(kernel, out_shape=shapes, in_specs=specs or [vmem] * len(a...  6.07 us
    ppermute x2, waiting for transfers between devices, butterfly(): return lax.ppermute(x, ('grp', 'dev'), pairs)  4.89 us
    ppermute x2, starting transfers between devices, butterfly(): return lax.ppermute(x, ('grp', 'dev'), pairs)  3.13 us
    add x1, other arithmetic, step(): total = part.astype(F32) + other.astype(F32)  0.86 us
  transfers between devices with their start and end apart: 15, of which 8 were waited for; matrix products, arithmetic and copies ran while one was open for 0% of the time, Pallas kernels for 12%

profile of v4, /device:TPU:0, one launch (start us, length us, event | category | flops | bytes accessed | tf_op | source)
XLA Modules:
  0.0 42.5 jit_solution(15521318747739672006)
XLA Ops:
  0.6 0.6 %collective-permute-start.4 = (bf16[512,256]{1,0:T(8,128)(2,1)}, bf16[512,256]{1,0:T(8,128)(2,1)S(1)}, u32[]{:S(2)}, u32[]{:S(2)}) collective-permute-start(bf16[512,256]{1,0:T(8,128)(2,1)} %r_4_.1), channel_id=1, source_target_pairs={{0,1},{1,0},{2,3},{3,2},{4,5},{5,4},{6,7},{7,6},{8,9},{9,8},{10,11... | collective-permute-start | bytes 786440 | tf_op jit(solution)/shard_map/ppermute | solution.py:20
  1.2 0.1 collective-permute-start.3
  1.3 3.0 %collective-permute-start = (bf16[128,256]{1,0:T(8,128)(2,1)}, bf16[128,256]{1,0:T(8,128)(2,1)S(1)}, u32[]{:S(2)}, u32[]{:S(2)}) collective-permute-start(bf16[128,256]{1,0:T(8,128)(2,1)} %r_2_.1), channel_id=1, source_target_pairs={{0,2},{1,3},{2,0},{3,1},{4,6},{5,7},{6,4},{7,5},{8,10},{9,11},{10,... | collective-permute-start | bytes 196616 | tf_op jit(solution)/shard_map/ppermute | solution.py:20
  4.3 2.5 %collective-permute-start.2 = (bf16[128,256]{1,0:T(8,128)(2,1)}, bf16[128,256]{1,0:T(8,128)(2,1)S(1)}, u32[]{:S(2)}, u32[]{:S(2)}) collective-permute-start(bf16[128,256]{1,0:T(8,128)(2,1)} %r_2_.1), channel_id=1, source_target_pairs={{0,6},{1,7},{2,4},{3,5},{4,2},{5,3},{6,0},{7,1},{8,14},{9,15},{10,... | collective-permute-start | bytes 196616 | tf_op jit(solution)/shard_map/ppermute | solution.py:20
  6.7 1.4 %collective-permute-done.5 = f32[512]{0:T(512)S(1)} collective-permute-done((f32[512]{0:T(512)}, f32[512]{0:T(512)S(1)}, u32[]{:S(2)}, u32[]{:S(2)}) %collective-permute-start.5) | collective-permute-done | bytes 2080 | tf_op jit(solution)/shard_map/ppermute | solution.py:20
  8.1 0.1 collective-permute-start.1
  8.2 1.7 %shard_map.93 = (bf16[128,256]{1,0:T(8,128)(2,1)S(1)}, bf16[128,256]{1,0:T(8,128)(2,1)S(1)}, bf16[512,256]{1,0:T(8,128)(2,1)S(1)}, f32[128,128]{1,0:T(8,128)S(1)}) custom-call(s32[1024]{0:T(1024)} %r_0_.1, f32[2048,128]{1,0:T(8,128)} %bitcast.5, bf16[128,256]{1,0:T(8,128)(2,1)} %r_2_.1, bf16[128,256]{1,0:T(8,128)(2,1)} %r_3_.1, bf16[512,256]{1,0:T(8,128)(2,1)} %r_4_.1, ...), custom_call_target="tpu_custom_call" | custom-call | flops 16384 | tf_op jit(solution)/shard_map/pallas_call | solution.py:263
  10.0 0.6 %shard_map.94 = (f32[3,128]{1,0:T(4,128)S(1)}, f32[1280,128]{1,0:T(8,128)S(1)}, bf16[256,1280]{1,0:T(8,128)(2,1)S(1)}, f32[128,128]{1,0:T(8,128)S(1)}) custom-call(bf16[128,256]{1,0:T(8,128)(2,1)S(1)} %get-tuple-element.38.q_ref.r_0_, bf16[128,256]{1,0:T(8,128)(2,1)S(1)} %get-tuple-element.39.it_o.r_2_.r_1_, ...), custom_call_target="tpu_custom_call" | custom-call | flops 83886080 | tf_op jit(solution)/shard_map/pallas_call | solution.py:263
  10.6 0.1 collective-permute-done.2.r_1_.r_3_
  10.7 1.0 %shard_map.95 = (f32[4,128]{1,0:T(4,128)S(1)}, f32[1280,128]{1,0:T(8,128)S(1)}, f32[1280,128]{1,0:T(8,128)S(1)}, bf16[256,128]{1,0:T(8,128)(2,1)S(1)}) custom-call(bf16[128,256]{1,0:T(8,128)(2,1)S(1)} %collective-permute-done.r_0_.r_1_, bf16[128,256]{1,0:T(8,128)(2,1)S(1)} %collective-permute-done.2.r_1_.r_3_, ...), custom_call_target="tpu_custom_call" | custom-call | flops 167772160 | tf_op jit(solution)/shard_map/pallas_call | solution.py:263
  11.7 3.1 %collective-permute-done.1.r_0_.r_2_ = bf16[128,256]{1,0:T(8,128)(2,1)S(1)} collective-permute-done((bf16[128,256]{1,0:T(8,128)(2,1)}, bf16[128,256]{1,0:T(8,128)(2,1)S(1)}, u32[]{:S(2)}, u32[]{:S(2)}) %collective-permute-start.1) | collective-permute-done | bytes 65568 | tf_op jit(solution)/shard_map/ppermute | solution.py:20
  14.8 0.5 %shard_map.96 = (f32[4,128]{1,0:T(4,128)S(1)}, f32[4,128]{1,0:T(4,128)S(1)}, bf16[16,128]{1,0:T(8,128)(2,1)S(1)}, bf16[272,128]{1,0:T(8,128)(2,1)S(1)}, f32[1280,128]{1,0:T(8,128)S(1)}) custom-call(bf16[128,256]{1,0:T(8,128)(2,1)S(1)} %collective-permute-done.1.r_0_.r_2_, bf16[128,256]{1,0:T(8,128)(2,1)S(1)} %get-tuple-element.39.it_o.r_2_.r_1_, ...), custom_call_target="tpu_custom_call" | custom-call | flops 83886080 | tf_op jit(solution)/shard_map/pallas_call | solution.py:263
  15.3 0.1 collective-permute-start.6
  15.4 1.5 %collective-permute-start.8 = (bf16[16,128]{1,0:T(8,128)(2,1)S(1)}, bf16[16,128]{1,0:T(8,128)(2,1)S(1)}, u32[]{:S(2)}, u32[]{:S(2)}) collective-permute-start(bf16[16,128]{1,0:T(8,128)(2,1)S(1)} %get-tuple-element.54), channel_id=1, source_target_pairs={{0,6},{1,7},{2,4},{3,5},{4,2},{5,3},{6,0},{7,1},{8,14},{9,15},{10,... | collective-permute-start | bytes 12296 | tf_op jit(solution)/shard_map/ppermute | solution.py:20
  16.9 1.9 %collective-permute-start.7 = (bf16[16,128]{1,0:T(8,128)(2,1)S(1)}, bf16[16,128]{1,0:T(8,128)(2,1)S(1)}, u32[]{:S(2)}, u32[]{:S(2)}) collective-permute-start(bf16[16,128]{1,0:T(8,128)(2,1)S(1)} %get-tuple-element.54), channel_id=1, source_target_pairs={{0,4},{1,5},{2,6},{3,7},{4,0},{5,1},{6,2},{7,3},{8,12},{9,13},{10,... | collective-permute-start | bytes 12296 | tf_op jit(solution)/shard_map/ppermute | solution.py:20
  18.8 2.0 %collective-permute-done.8.r_13_ = bf16[16,128]{1,0:T(8,128)(2,1)S(1)} collective-permute-done((bf16[16,128]{1,0:T(8,128)(2,1)S(1)}, bf16[16,128]{1,0:T(8,128)(2,1)S(1)}, u32[]{:S(2)}, u32[]{:S(2)}) %collective-permute-start.8) | collective-permute-done | bytes 4128 | tf_op jit(solution)/shard_map/ppermute | solution.py:20
  20.8 0.6 %collective-permute-done.7.r_12_ = bf16[16,128]{1,0:T(8,128)(2,1)S(1)} collective-permute-done((bf16[16,128]{1,0:T(8,128)(2,1)S(1)}, bf16[16,128]{1,0:T(8,128)(2,1)S(1)}, u32[]{:S(2)}, u32[]{:S(2)}) %collective-permute-start.7) | collective-permute-done | bytes 4128 | tf_op jit(solution)/shard_map/ppermute | solution.py:20
  21.4 0.4 shard_map.97
  21.8 0.1 collective-permute-start.12
  21.9 0.4 shard_map.98
  22.3 1.1 %collective-permute-done.12 = bf16[512,256]{1,0:T(8,128)(2,1)S(1)} collective-permute-done((bf16[512,256]{1,0:T(8,128)(2,1)S(1)}, bf16[512,256]{1,0:T(8,128)(2,1)S(1)}, u32[]{:S(2)}, u32[]{:S(2)}) %collective-permute-start.12) | collective-permute-done | bytes 262176 | tf_op jit(solution)/shard_map/ppermute | solution.py:20
  23.4 0.1 add_convert_fusion.1
  23.4 1.5 %collective-permute-start.13 = (bf16[512,256]{1,0:T(8,128)(2,1)S(1)}, bf16[512,256]{1,0:T(8,128)(2,1)S(1)}, u32[]{:S(2)}, u32[]{:S(2)}) collective-permute-start(bf16[512,256]{1,0:T(8,128)(2,1)S(1)} %add_convert_fusion.1), channel_id=1, source_target_pairs={{0,8},{1,17},{2,10},{3,19},{4,12},{5,21},{6,14},{7,23},{8,0},{9,25... | collective-permute-start | bytes 786440 | tf_op jit(solution)/shard_map/ppermute | solution.py:280
  25.0 4.9 %collective-permute-done.13 = bf16[512,256]{1,0:T(8,128)(2,1)S(1)} collective-permute-done((bf16[512,256]{1,0:T(8,128)(2,1)S(1)}, bf16[512,256]{1,0:T(8,128)(2,1)S(1)}, u32[]{:S(2)}, u32[]{:S(2)}) %collective-permute-start.13) | collective-permute-done | bytes 262176 | tf_op jit(solution)/shard_map/ppermute | solution.py:280
  29.9 0.1 add_convert_fusion
  29.9 1.6 %collective-permute-start.14 = (bf16[512,256]{1,0:T(8,128)(2,1)S(1)}, bf16[512,256]{1,0:T(8,128)(2,1)S(1)}, u32[]{:S(2)}, u32[]{:S(2)}) collective-permute-start(bf16[512,256]{1,0:T(8,128)(2,1)S(1)} %add_convert_fusion), channel_id=1, source_target_pairs={{0,16},{1,9},{2,18},{3,11},{4,20},{5,13},{6,22},{7,15},{8,24},{9,1... | collective-permute-start | bytes 786440 | tf_op jit(solution)/shard_map/ppermute | solution.py:280
  31.5 0.7 %shard_map.99 = (f32[256,128]{1,0:T(8,128)S(1)}, bf16[256,128]{1,0:T(8,128)(2,1)S(1)}, bf16[256,128]{1,0:T(8,128)(2,1)S(1)}) custom-call(bf16[256,1280]{1,0:T(8,128)(2,1)S(1)} %get-tuple-element.44.r_8_.r_0_, bf16[256,512]{1,0:T(8,128)(2,1)S(1)} %get-tuple-element.60.r_1_, bf16[512,512]{1,0:T(8,128)(2,1)S(1)} %get-tuple-element.61.r_2_, ...), custom_call_target="tpu_custom_call" | custom-call | flops 251658240 | tf_op jit(solution)/shard_map/pallas_call | solution.py:263
  32.2 2.0 %collective-permute-start.10 = (bf16[256,128]{1,0:T(8,128)(2,1)S(1)}, bf16[256,128]{1,0:T(8,128)(2,1)S(1)}, u32[]{:S(2)}, u32[]{:S(2)}) collective-permute-start(bf16[256,128]{1,0:T(8,128)(2,1)S(1)} %get-tuple-element.65), channel_id=1, source_target_pairs={{0,4},{1,5},{2,6},{3,7},{4,0},{5,1},{6,2},{7,3},{8,12},{9,13},{10,... | collective-permute-start | bytes 196616 | tf_op jit(solution)/shard_map/ppermute | solution.py:20
  34.2 1.3 %collective-permute-start.11 = (bf16[256,128]{1,0:T(8,128)(2,1)S(1)}, bf16[256,128]{1,0:T(8,128)(2,1)S(1)}, u32[]{:S(2)}, u32[]{:S(2)}) collective-permute-start(bf16[256,128]{1,0:T(8,128)(2,1)S(1)} %get-tuple-element.66), channel_id=1, source_target_pairs={{0,6},{1,7},{2,4},{3,5},{4,2},{5,3},{6,0},{7,1},{8,14},{9,15},{10,... | collective-permute-start | bytes 196616 | tf_op jit(solution)/shard_map/ppermute | solution.py:20
  35.5 5.4 %collective-permute-done.10.refs_0_ = bf16[256,128]{1,0:T(8,128)(2,1)S(1)} collective-permute-done((bf16[256,128]{1,0:T(8,128)(2,1)S(1)}, bf16[256,128]{1,0:T(8,128)(2,1)S(1)}, u32[]{:S(2)}, u32[]{:S(2)}) %collective-permute-start.10) | collective-permute-done | bytes 65568 | tf_op jit(solution)/shard_map/ppermute | solution.py:20
  40.8 0.8 %shard_map.100 = (f32[1,128]{1,0:T(1,128)}, f32[128,256]{1,0:T(8,128)}, f32[128,256]{1,0:T(8,128)}) custom-call(f32[1,128]{1,0:T(1,128)S(1)} %get-tuple-element.55.loss_in, f32[128,256]{1,0:T(8,128)S(1)} %get-tuple-element.58.mine_ref, bf16[128,256]{1,0:T(8,128)(2,1)S(1)} %collective-permute-done.9.back_ref, f32[256,128]{1,0:T(8,128)S(1)} %get-tuple-element.63.own_ref, ...), custom_call_target="tpu_custom_call" | custom-call | flops 131072 | tf_op jit(solution)/shard_map/pallas_call | solution.py:263
  41.7 0.9 %convert_add_fusion = f32[512,256]{1,0:T(8,128)} fusion(bf16[512,256]{1,0:T(8,128)(2,1)S(1)} %collective-permute-done.14, bf16[512,256]{1,0:T(8,128)(2,1)S(1)} %add_convert_fusion), kind=kLoop, calls=%fused_computation | loop fusion | flops 393216 | bytes 1048576 | tf_op jit(solution)/shard_map/add | solution.py:411
  (9 shorter events, 0.0 us)
Async XLA Ops:
  0.6 9.3 %collective-permute-start.4 = (bf16[512,256]{1,0:T(8,128)(2,1)}, bf16[512,256]{1,0:T(8,128)(2,1)S(1)}, u32[]{:S(2)}, u32[]{:S(2)}) collective-permute-start(bf16[512,256]{1,0:T(8,128)(2,1)} %r_4_.1), channel_id=1, source_target_pairs={{0,1},{1,0},{2,3},{3,2},{4,5},{5,4},{6,7},{7,6},{8,9},{9,8},{10,11... | collective-permute-start | bytes 786440 | tf_op jit(solution)/shard_map/ppermute | solution.py:20
  1.2 8.8 %collective-permute-start.3 = (bf16[128,256]{1,0:T(8,128)(2,1)}, bf16[128,256]{1,0:T(8,128)(2,1)S(1)}, u32[]{:S(2)}, u32[]{:S(2)}) collective-permute-start(bf16[128,256]{1,0:T(8,128)(2,1)} %r_3_.1), channel_id=1, source_target_pairs={{0,1},{1,0},{2,3},{3,2},{4,5},{5,4},{6,7},{7,6},{8,9},{9,8},{10,11... | collective-permute-start | bytes 196616 | tf_op jit(solution)/shard_map/ppermute | solution.py:20
  1.3 9.3 %collective-permute-start = (bf16[128,256]{1,0:T(8,128)(2,1)}, bf16[128,256]{1,0:T(8,128)(2,1)S(1)}, u32[]{:S(2)}, u32[]{:S(2)}) collective-permute-start(bf16[128,256]{1,0:T(8,128)(2,1)} %r_2_.1), channel_id=1, source_target_pairs={{0,2},{1,3},{2,0},{3,1},{4,6},{5,7},{6,4},{7,5},{8,10},{9,11},{10,... | collective-permute-start | bytes 196616 | tf_op jit(solution)/shard_map/ppermute | solution.py:20
  4.3 6.4 %collective-permute-start.2 = (bf16[128,256]{1,0:T(8,128)(2,1)}, bf16[128,256]{1,0:T(8,128)(2,1)S(1)}, u32[]{:S(2)}, u32[]{:S(2)}) collective-permute-start(bf16[128,256]{1,0:T(8,128)(2,1)} %r_2_.1), channel_id=1, source_target_pairs={{0,6},{1,7},{2,4},{3,5},{4,2},{5,3},{6,0},{7,1},{8,14},{9,15},{10,... | collective-permute-start | bytes 196616 | tf_op jit(solution)/shard_map/ppermute | solution.py:20
  6.7 1.4 %collective-permute-start.5 = (f32[512]{0:T(512)}, f32[512]{0:T(512)S(1)}, u32[]{:S(2)}, u32[]{:S(2)}) collective-permute-start(f32[512]{0:T(512)} %param.10), channel_id=1, source_target_pairs={{0,1},{1,0},{2,3},{3,2},{4,5},{5,4},{6,7},{7,6},{8,9},{9,8},{10,11... | collective-permute-start | bytes 6152 | tf_op jit(solution)/shard_map/ppermute | solution.py:20
  8.1 6.7 %collective-permute-start.1 = (bf16[128,256]{1,0:T(8,128)(2,1)}, bf16[128,256]{1,0:T(8,128)(2,1)S(1)}, u32[]{:S(2)}, u32[]{:S(2)}) collective-permute-start(bf16[128,256]{1,0:T(8,128)(2,1)} %r_2_.1), channel_id=1, source_target_pairs={{0,4},{1,5},{2,6},{3,7},{4,0},{5,1},{6,2},{7,3},{8,12},{9,13},{10,... | collective-permute-start | bytes 196616 | tf_op jit(solution)/shard_map/ppermute | solution.py:20
  15.3 6.1 %collective-permute-start.6 = (bf16[272,128]{1,0:T(8,128)(2,1)S(1)}, bf16[272,128]{1,0:T(8,128)(2,1)S(1)}, u32[]{:S(2)}, u32[]{:S(2)}) collective-permute-start(bf16[272,128]{1,0:T(8,128)(2,1)S(1)} %get-tuple-element.53), channel_id=1, source_target_pairs={{0,2},{1,3},{2,0},{3,1},{4,6},{5,7},{6,4},{7,5},{8,10},{9,11},{10,... | collective-permute-start | bytes 208904 | tf_op jit(solution)/shard_map/ppermute | solution.py:20
  15.4 5.5 %collective-permute-start.8 = (bf16[16,128]{1,0:T(8,128)(2,1)S(1)}, bf16[16,128]{1,0:T(8,128)(2,1)S(1)}, u32[]{:S(2)}, u32[]{:S(2)}) collective-permute-start(bf16[16,128]{1,0:T(8,128)(2,1)S(1)} %get-tuple-element.54), channel_id=1, source_target_pairs={{0,6},{1,7},{2,4},{3,5},{4,2},{5,3},{6,0},{7,1},{8,14},{9,15},{10,... | collective-permute-start | bytes 12296 | tf_op jit(solution)/shard_map/ppermute | solution.py:20
  16.9 4.5 %collective-permute-start.7 = (bf16[16,128]{1,0:T(8,128)(2,1)S(1)}, bf16[16,128]{1,0:T(8,128)(2,1)S(1)}, u32[]{:S(2)}, u32[]{:S(2)}) collective-permute-start(bf16[16,128]{1,0:T(8,128)(2,1)S(1)} %get-tuple-element.54), channel_id=1, source_target_pairs={{0,4},{1,5},{2,6},{3,7},{4,0},{5,1},{6,2},{7,3},{8,12},{9,13},{10,... | collective-permute-start | bytes 12296 | tf_op jit(solution)/shard_map/ppermute | solution.py:20
  21.8 1.6 %collective-permute-start.12 = (bf16[512,256]{1,0:T(8,128)(2,1)S(1)}, bf16[512,256]{1,0:T(8,128)(2,1)S(1)}, u32[]{:S(2)}, u32[]{:S(2)}) collective-permute-start(bf16[512,256]{1,0:T(8,128)(2,1)S(1)} %get-tuple-element.71), channel_id=1, source_target_pairs={{0,1},{1,0},{2,3},{3,2},{4,5},{5,4},{6,7},{7,6},{8,9},{9,8},{10,11... | collective-permute-start | bytes 786440 | tf_op jit(solution)/shard_map/ppermute | solution.py:20
  23.4 6.4 %collective-permute-start.13 = (bf16[512,256]{1,0:T(8,128)(2,1)S(1)}, bf16[512,256]{1,0:T(8,128)(2,1)S(1)}, u32[]{:S(2)}, u32[]{:S(2)}) collective-permute-start(bf16[512,256]{1,0:T(8,128)(2,1)S(1)} %add_convert_fusion.1), channel_id=1, source_target_pairs={{0,8},{1,17},{2,10},{3,19},{4,12},{5,21},{6,14},{7,23},{8,0},{9,25... | collective-permute-start | bytes 786440 | tf_op jit(solution)/shard_map/ppermute | solution.py:280
  29.9 11.7 %collective-permute-start.14 = (bf16[512,256]{1,0:T(8,128)(2,1)S(1)}, bf16[512,256]{1,0:T(8,128)(2,1)S(1)}, u32[]{:S(2)}, u32[]{:S(2)}) collective-permute-start(bf16[512,256]{1,0:T(8,128)(2,1)S(1)} %add_convert_fusion), channel_id=1, source_target_pairs={{0,16},{1,9},{2,18},{3,11},{4,20},{5,13},{6,22},{7,15},{8,24},{9,1... | collective-permute-start | bytes 786440 | tf_op jit(solution)/shard_map/ppermute | solution.py:280
  31.5 3.9 %collective-permute-start.9 = (bf16[128,256]{1,0:T(8,128)(2,1)S(1)}, bf16[128,256]{1,0:T(8,128)(2,1)S(1)}, u32[]{:S(2)}, u32[]{:S(2)}) collective-permute-start(bf16[128,256]{1,0:T(8,128)(2,1)S(1)} %get-tuple-element.59), channel_id=1, source_target_pairs={{0,1},{1,0},{2,3},{3,2},{4,5},{5,4},{6,7},{7,6},{8,9},{9,8},{10,11... | collective-permute-start | bytes 196616 | tf_op jit(solution)/shard_map/ppermute | solution.py:20
  32.2 8.6 %collective-permute-start.10 = (bf16[256,128]{1,0:T(8,128)(2,1)S(1)}, bf16[256,128]{1,0:T(8,128)(2,1)S(1)}, u32[]{:S(2)}, u32[]{:S(2)}) collective-permute-start(bf16[256,128]{1,0:T(8,128)(2,1)S(1)} %get-tuple-element.65), channel_id=1, source_target_pairs={{0,4},{1,5},{2,6},{3,7},{4,0},{5,1},{6,2},{7,3},{8,12},{9,13},{10,... | collective-permute-start | bytes 196616 | tf_op jit(solution)/shard_map/ppermute | solution.py:20
  34.2 6.6 %collective-permute-start.11 = (bf16[256,128]{1,0:T(8,128)(2,1)S(1)}, bf16[256,128]{1,0:T(8,128)(2,1)S(1)}, u32[]{:S(2)}, u32[]{:S(2)}) collective-permute-start(bf16[256,128]{1,0:T(8,128)(2,1)S(1)} %get-tuple-element.66), channel_id=1, source_target_pairs={{0,6},{1,7},{2,4},{3,5},{4,2},{5,3},{6,0},{7,1},{8,14},{9,15},{10,... | collective-permute-start | bytes 196616 | tf_op jit(solution)/shard_map/ppermute | solution.py:20
